TPU v7x, 32 devices: a whole 2x2x4 slice. The times are simulated.
32 devices in a mesh: dp: 16 (over z, y, x), tensor: 2 (over core).
Axes of the slice: x: 2, y: 2, z: 4, core: 2. Of those that a mesh axis runs over, the one named last changes fastest.
Arguments:
- src: bfloat16 [16, 1024, 1024], P('dp', 'tensor'), may hold values from -6 to 6
- tgt: bfloat16 [16, 1024, 1024], P('dp', 'tensor'), may hold values from -6 to 6
- src_len: int32 [16], P('dp'), may hold values from 256 to 1024, as said below
- tgt_len: int32 [16], P('dp'), may hold values from 256 to 1024, as said below
- enc_qkv: bfloat16 [3, 1024, 1024], P(None, None, 'tensor'), may hold values from -0.1875 to 0.1875
- enc_out_w: bfloat16 [1024, 1024], P('tensor'), may hold values from -1.5 to 1.5
- enc_ffn_in: bfloat16 [1024, 4096], P(None, 'tensor'), may hold values from -0.1875 to 0.1875
- enc_ffn_out: bfloat16 [4096, 1024], P('tensor'), may hold values from -0.09375 to 0.09375
- enc_gain: float32 [3, 1024], replicated, may hold values from 0.25 to 1.75
- enc_bias: float32 [3, 1024], replicated, may hold values from -1.5 to 1.5
- dec_qkv: bfloat16 [3, 1024, 1024], P(None, None, 'tensor'), may hold values from -0.1875 to 0.1875
- dec_self_out: bfloat16 [1024, 1024], P('tensor'), may hold values from -1.5 to 1.5
- dec_cross: bfloat16 [3, 1024, 1024], P(None, None, 'tensor'), may hold values from -0.1875 to 0.1875
- dec_cross_out: bfloat16 [1024, 1024], P('tensor'), may hold values from -1.5 to 1.5
- dec_ffn_in: bfloat16 [1024, 4096], P(None, 'tensor'), may hold values from -0.1875 to 0.1875
- dec_ffn_out: bfloat16 [4096, 1024], P('tensor'), may hold values from -0.09375 to 0.09375
- dec_gain: float32 [4, 1024], replicated, may hold values from 0.25 to 1.75
- dec_bias: float32 [4, 1024], replicated, may hold values from -1.5 to 1.5
- enc_cot: bfloat16 [16, 1024, 1024], P('dp', 'tensor'), may hold values from -6 to 6
- dec_cot: bfloat16 [16, 1024, 1024], P('dp', 'tensor'), may hold values from -6 to 6
Outputs:
- enc_out: bfloat16 [16, 1024, 1024], P('dp', 'tensor')
- dec_out: bfloat16 [16, 1024, 1024], P('dp', 'tensor')
- grad_src: float32 [16, 1024, 1024], P('dp', 'tensor')
- grad_tgt: float32 [16, 1024, 1024], P('dp', 'tensor')
- enc_qkv_grad: float32 [3, 1024, 1024], P(None, None, 'tensor')
- enc_out_w_grad: float32 [1024, 1024], P('tensor')
- enc_ffn_in_grad: float32 [1024, 4096], P(None, 'tensor')
- enc_ffn_out_grad: float32 [4096, 1024], P('tensor')
- enc_gain_grad: float32 [3, 1024], replicated
- enc_bias_grad: float32 [3, 1024], replicated
- dec_qkv_grad: float32 [3, 1024, 1024], P(None, None, 'tensor')
- dec_self_out_grad: float32 [1024, 1024], P('tensor')
- dec_cross_grad: float32 [3, 1024, 1024], P(None, None, 'tensor')
- dec_cross_out_grad: float32 [1024, 1024], P('tensor')
- dec_ffn_in_grad: float32 [1024, 4096], P(None, 'tensor')
- dec_ffn_out_grad: float32 [4096, 1024], P('tensor')
- dec_gain_grad: float32 [4, 1024], replicated
- dec_bias_grad: float32 [4, 1024], replicated
Inputs may be any that keep to these rules, and one draw needn't show every extreme that they name: The first src_len[b] positions of pair b's source are filled and the rest is padding; in every draw some pair has a full source of 1024. `tgt_len`: likewise for the target positions; in every draw some pair has a full target of 1024.
All inputs are finite; a program needn't handle non-finite values.
Results may differ from a plain program's by a relative error of at most 0.022.
Values may be sent and summed in bfloat16 or wider, within the bound.
No kernel may reach another device: no remote copies, remote signals or barrier semaphores. Data moves between devices by JAX's collectives and lax.ppermute only.
A program may use at most 448 MiB of HBM per device.

v0:
```python
import math

import jax
import jax.numpy as jnp
from jax import lax
from jax.sharding import PartitionSpec as P

HEAD_DIM = 64
QBLK = 512


epsilon = 1e-05
root_half = 1.0 / math.sqrt(2.0)
root_two_pi = 1.0 / math.sqrt(2.0 * math.pi)


def norm_forward(hidden, gain, shift):
    center = hidden - jnp.mean(hidden, axis=-1, keepdims=True)
    inverse = lax.rsqrt(jnp.mean(center * center, axis=-1, keepdims=True) + epsilon)
    normed = center * inverse
    return (normed * gain + shift, normed, inverse)


def norm_backward(grad, normed, inverse, gain):
    scaled = grad * gain
    inner = (
        scaled
        - jnp.mean(scaled, axis=-1, keepdims=True)
        - normed * jnp.mean(scaled * normed, axis=-1, keepdims=True)
    )
    return (inverse * inner, jnp.sum(grad * normed, axis=(0, 1)), jnp.sum(grad, axis=(0, 1)))


def gelu_value(zed):
    return 0.5 * zed * (1.0 + lax.erf(zed * root_half))


def gelu_slope(zed):
    return 0.5 * (1.0 + lax.erf(zed * root_half)) + zed * jnp.exp(-0.5 * zed * zed) * root_two_pi


def project(left, weight):
    return jnp.einsum("psd,dh->psh", left, weight, preferred_element_type=jnp.float32)


def back_project(grad, weight):
    return jnp.einsum("psh,dh->psd", grad, weight, preferred_element_type=jnp.float32)


def weight_grad(left, grad):
    return jnp.einsum("psd,psh->dh", left, grad, preferred_element_type=jnp.float32)


def spread(stacked):
    return lax.all_gather(stacked, "tensor", axis=2, tiled=True)


def collect(partial_rows):
    return lax.psum_scatter(
        partial_rows.astype(jnp.bfloat16), "tensor", scatter_dimension=1, tiled=True
    ).astype(jnp.float32)


def spread_grad(grad):
    return lax.all_gather(grad.astype(jnp.bfloat16), "tensor", axis=1, tiled=True)


def collect_grad(stacked):
    return lax.psum_scatter(
        stacked.astype(jnp.bfloat16), "tensor", scatter_dimension=2, tiled=True
    ).astype(jnp.float32)


def split_heads(value):
    return value.reshape(value.shape[0], value.shape[1], value.shape[2] // HEAD_DIM, HEAD_DIM)


def key_mask(key_len, start, length, causal):
    key_pos = jnp.arange(length)
    allowed = (key_pos[None, :] < key_len[:, None])[:, None, None, :]
    if causal:
        query_pos = start + jnp.arange(QBLK)
        allowed = allowed & (key_pos[None, :] <= query_pos[:, None])[None, None]
    return allowed


def block_scores(query_block, keys, allowed):
    raw = jnp.einsum("pqhd,pkhd->phqk", query_block, keys, preferred_element_type=jnp.float32)
    return jnp.where(allowed, raw * HEAD_DIM ** (-0.5), -1e30)


def attend_forward(queries, keys, values, key_len, causal):
    length = queries.shape[1]
    contexts = []
    log_parts = []
    for block_index in range(length // QBLK):
        start = block_index * QBLK
        query_block = queries[:, start : start + QBLK]
        scores = block_scores(query_block, keys, key_mask(key_len, start, length, causal))
        row_top = jnp.max(scores, axis=-1, keepdims=True)
        exp_scores = jnp.exp(scores - row_top)
        row_total = jnp.sum(exp_scores, axis=-1, keepdims=True)
        soft_block = (exp_scores / row_total).astype(jnp.bfloat16)
        contexts.append(
            jnp.einsum("phqk,pkhd->pqhd", soft_block, values, preferred_element_type=jnp.float32)
        )
        log_parts.append(row_top + jnp.log(row_total))
    return (jnp.concatenate(contexts, axis=1), jnp.concatenate(log_parts, axis=2))


def attend_backward(queries, keys, values, log_sums, grad_context, key_len, causal):
    length = queries.shape[1]
    grad_queries = []
    grad_keys = jnp.zeros(keys.shape, jnp.float32)
    grad_values = jnp.zeros(values.shape, jnp.float32)
    for block_index in range(length // QBLK):
        start = block_index * QBLK
        query_block = queries[:, start : start + QBLK]
        grad_block = grad_context[:, start : start + QBLK]
        scores = block_scores(query_block, keys, key_mask(key_len, start, length, causal))
        soft_block = jnp.exp(scores - log_sums[:, :, start : start + QBLK])
        grad_soft = jnp.einsum(
            "pqhd,pkhd->phqk", grad_block, values, preferred_element_type=jnp.float32
        )
        row_dot = jnp.sum(soft_block * grad_soft, axis=-1, keepdims=True)
        grad_scores = (soft_block * (grad_soft - row_dot) * HEAD_DIM ** (-0.5)).astype(jnp.bfloat16)
        grad_queries.append(
            jnp.einsum("phqk,pkhd->pqhd", grad_scores, keys, preferred_element_type=jnp.float32)
        )
        grad_keys = grad_keys + jnp.einsum(
            "phqk,pqhd->pkhd", grad_scores, query_block, preferred_element_type=jnp.float32
        )
        grad_values = grad_values + jnp.einsum(
            "phqk,pqhd->pkhd",
            soft_block.astype(jnp.bfloat16),
            grad_block,
            preferred_element_type=jnp.float32,
        )
    return (jnp.concatenate(grad_queries, axis=1), grad_keys, grad_values)


def attention_forward(query_in, memory_in, w_query, w_key, w_value, w_out, key_len, causal):
    queries = project(query_in, w_query).astype(jnp.bfloat16)
    keys = project(memory_in, w_key).astype(jnp.bfloat16)
    values = project(memory_in, w_value).astype(jnp.bfloat16)
    context, log_sums = attend_forward(
        split_heads(queries), split_heads(keys), split_heads(values), key_len, causal
    )
    context = context.reshape(queries.shape).astype(jnp.bfloat16)
    return (collect(project(context, w_out)), (queries, keys, values, context, log_sums))


def attention_backward(
    grad_out, query_in, memory_in, w_query, w_key, w_value, w_out, kept, key_len, causal
):
    queries, keys, values, context, log_sums = kept
    grad_full = spread_grad(grad_out)
    grad_w_out = weight_grad(context, grad_full)
    grad_context = back_project(grad_full, w_out).astype(jnp.bfloat16)
    grad_q, grad_k, grad_v = attend_backward(
        split_heads(queries),
        split_heads(keys),
        split_heads(values),
        log_sums,
        split_heads(grad_context),
        key_len,
        causal,
    )
    grad_q = grad_q.reshape(queries.shape).astype(jnp.bfloat16)
    grad_k = grad_k.reshape(keys.shape).astype(jnp.bfloat16)
    grad_v = grad_v.reshape(values.shape).astype(jnp.bfloat16)
    weight_grads = (
        weight_grad(query_in, grad_q),
        weight_grad(memory_in, grad_k),
        weight_grad(memory_in, grad_v),
        grad_w_out,
    )
    from_query = back_project(grad_q, w_query)
    from_memory = back_project(grad_k, w_key) + back_project(grad_v, w_value)
    return (weight_grads, from_query, from_memory)


def ffn_forward(normed_rows, w_in, w_out):
    rows_full = spread(normed_rows[None])[0]
    zed = project(rows_full, w_in)
    unit = gelu_value(zed).astype(jnp.bfloat16)
    result = collect(project(unit, w_out))
    kept = (rows_full, zed, unit, w_in, w_out)
    return (result, kept)


def ffn_backward(grad_out, kept):
    rows, zed, unit, w_in, w_out = kept
    grad_full = spread_grad(grad_out)
    grad_w_out = weight_grad(unit, grad_full)
    grad_unit = back_project(grad_full, w_out).astype(jnp.bfloat16)
    grad_zed = (grad_unit.astype(jnp.float32) * gelu_slope(zed)).astype(jnp.bfloat16)
    grad_w_in = weight_grad(rows, grad_zed)
    grad_rows = back_project(grad_zed, w_in)
    grad_input = collect_grad(grad_rows[None])[0]
    return (grad_input, grad_w_in, grad_w_out)


def on_device(
    src,
    tgt,
    src_len,
    tgt_len,
    enc_qkv,
    enc_out_w,
    enc_ffn_in,
    enc_ffn_out,
    enc_gain,
    enc_bias,
    dec_qkv,
    dec_self_out,
    dec_cross,
    dec_cross_out,
    dec_ffn_in,
    dec_ffn_out,
    dec_gain,
    dec_bias,
    enc_cot,
    dec_cot,
):
    source = src.astype(jnp.float32)
    ln_a1, nm_a1, inv_a1 = norm_forward(source, enc_gain[0], enc_bias[0])
    enc_rows = spread(ln_a1.astype(jnp.bfloat16)[None])[0]
    attn_enc, keep_enc_attn = attention_forward(
        enc_rows, enc_rows, enc_qkv[0], enc_qkv[1], enc_qkv[2], enc_out_w, src_len, False
    )
    hidden_one = source + attn_enc
    ln_a2, nm_a2, inv_a2 = norm_forward(hidden_one, enc_gain[1], enc_bias[1])
    ffn_enc, keep_enc_ffn = ffn_forward(ln_a2.astype(jnp.bfloat16), enc_ffn_in, enc_ffn_out)
    hidden_two = hidden_one + ffn_enc
    ln_mem, nm_mem, inv_mem = norm_forward(hidden_two, enc_gain[2], enc_bias[2])
    memory = ln_mem.astype(jnp.bfloat16)
    target = tgt.astype(jnp.float32)
    ln_b1, nm_b1, inv_b1 = norm_forward(target, dec_gain[0], dec_bias[0])
    dec_rows = spread(ln_b1.astype(jnp.bfloat16)[None])[0]
    attn_self, keep_self = attention_forward(
        dec_rows, dec_rows, dec_qkv[0], dec_qkv[1], dec_qkv[2], dec_self_out, tgt_len, True
    )
    resid_one = target + attn_self
    ln_b2, nm_b2, inv_b2 = norm_forward(resid_one, dec_gain[1], dec_bias[1])
    gathered = spread(jnp.stack([ln_b2.astype(jnp.bfloat16), memory]))
    cross_rows, memory_rows = (gathered[0], gathered[1])
    attn_cross, keep_cross = attention_forward(
        cross_rows,
        memory_rows,
        dec_cross[0],
        dec_cross[1],
        dec_cross[2],
        dec_cross_out,
        src_len,
        False,
    )
    resid_two = resid_one + attn_cross
    ln_b3, nm_b3, inv_b3 = norm_forward(resid_two, dec_gain[2], dec_bias[2])
    ffn_dec, keep_dec_ffn = ffn_forward(ln_b3.astype(jnp.bfloat16), dec_ffn_in, dec_ffn_out)
    resid_three = resid_two + ffn_dec
    ln_final, nm_final, inv_final = norm_forward(resid_three, dec_gain[3], dec_bias[3])
    grad_r3, gain_final, bias_final = norm_backward(
        dec_cot.astype(jnp.float32), nm_final, inv_final, dec_gain[3]
    )
    grad_b3, grad_dec_in, grad_dec_out = ffn_backward(grad_r3, keep_dec_ffn)
    part_r2, gain_b3, bias_b3 = norm_backward(grad_b3, nm_b3, inv_b3, dec_gain[2])
    grad_r2 = grad_r3 + part_r2
    cross_grads, from_query, from_memory = attention_backward(
        grad_r2,
        cross_rows,
        memory_rows,
        dec_cross[0],
        dec_cross[1],
        dec_cross[2],
        dec_cross_out,
        keep_cross,
        src_len,
        False,
    )
    summed_cross = collect_grad(jnp.stack([from_query, from_memory]))
    part_r1, gain_b2, bias_b2 = norm_backward(summed_cross[0], nm_b2, inv_b2, dec_gain[1])
    grad_r1 = grad_r2 + part_r1
    self_grads, self_query, self_memory = attention_backward(
        grad_r1,
        dec_rows,
        dec_rows,
        dec_qkv[0],
        dec_qkv[1],
        dec_qkv[2],
        dec_self_out,
        keep_self,
        tgt_len,
        True,
    )
    grad_b1 = collect_grad((self_query + self_memory)[None])[0]
    part_tgt, gain_b1, bias_b1 = norm_backward(grad_b1, nm_b1, inv_b1, dec_gain[0])
    grad_tgt = grad_r1 + part_tgt
    dec_grads = (
        jnp.stack(self_grads[:3]),
        self_grads[3],
        jnp.stack(cross_grads[:3]),
        cross_grads[3],
        grad_dec_in,
        grad_dec_out,
    )
    grad_memory = enc_cot.astype(jnp.float32) + summed_cross[1]
    grad_h2, gain_mem, bias_mem = norm_backward(grad_memory, nm_mem, inv_mem, enc_gain[2])
    grad_a2, grad_enc_in, grad_enc_out = ffn_backward(grad_h2, keep_enc_ffn)
    part_h1, gain_a2, bias_a2 = norm_backward(grad_a2, nm_a2, inv_a2, enc_gain[1])
    grad_h1 = grad_h2 + part_h1
    enc_grads_attn, enc_query, enc_memory = attention_backward(
        grad_h1,
        enc_rows,
        enc_rows,
        enc_qkv[0],
        enc_qkv[1],
        enc_qkv[2],
        enc_out_w,
        keep_enc_attn,
        src_len,
        False,
    )
    grad_a1 = collect_grad((enc_query + enc_memory)[None])[0]
    part_src, gain_a1, bias_a1 = norm_backward(grad_a1, nm_a1, inv_a1, enc_gain[0])
    grad_src = grad_h1 + part_src
    enc_grads = (jnp.stack(enc_grads_attn[:3]), enc_grads_attn[3], grad_enc_in, grad_enc_out)
    summed_all = (
        lax.psum(enc_grads[0].astype(jnp.bfloat16), "dp").astype(jnp.float32),
        lax.psum(enc_grads[1].astype(jnp.bfloat16), "dp").astype(jnp.float32),
        lax.psum(enc_grads[2].astype(jnp.bfloat16), "dp").astype(jnp.float32),
        lax.psum(enc_grads[3].astype(jnp.bfloat16), "dp").astype(jnp.float32),
        lax.psum(dec_grads[0].astype(jnp.bfloat16), "dp").astype(jnp.float32),
        lax.psum(dec_grads[1].astype(jnp.bfloat16), "dp").astype(jnp.float32),
        lax.psum(dec_grads[2].astype(jnp.bfloat16), "dp").astype(jnp.float32),
        lax.psum(dec_grads[3].astype(jnp.bfloat16), "dp").astype(jnp.float32),
        lax.psum(dec_grads[4].astype(jnp.bfloat16), "dp").astype(jnp.float32),
        lax.psum(dec_grads[5].astype(jnp.bfloat16), "dp").astype(jnp.float32),
    )
    enc_grads = summed_all[:4]
    dec_grads = summed_all[4:]
    enc_gain_grad, enc_bias_grad, dec_gain_grad, dec_bias_grad = lax.psum(
        (
            jnp.stack([gain_a1, gain_a2, gain_mem]),
            jnp.stack([bias_a1, bias_a2, bias_mem]),
            jnp.stack([gain_b1, gain_b2, gain_b3, gain_final]),
            jnp.stack([bias_b1, bias_b2, bias_b3, bias_final]),
        ),
        ("dp", "tensor"),
    )
    return (
        memory,
        ln_final.astype(jnp.bfloat16),
        grad_src,
        grad_tgt,
        enc_grads[0],
        enc_grads[1],
        enc_grads[2],
        enc_grads[3],
        enc_gain_grad,
        enc_bias_grad,
        dec_grads[0],
        dec_grads[1],
        dec_grads[2],
        dec_grads[3],
        dec_grads[4],
        dec_grads[5],
        dec_gain_grad,
        dec_bias_grad,
    )


def solution(mesh):
    in_specs = (
        P("dp", "tensor", None),
        P("dp", "tensor", None),
        P("dp"),
        P("dp"),
        P(None, None, "tensor"),
        P("tensor", None),
        P(None, "tensor"),
        P("tensor", None),
        P(),
        P(),
        P(None, None, "tensor"),
        P("tensor", None),
        P(None, None, "tensor"),
        P("tensor", None),
        P(None, "tensor"),
        P("tensor", None),
        P(),
        P(),
        P("dp", "tensor", None),
        P("dp", "tensor", None),
    )
    out_specs = (
        P("dp", "tensor", None),
        P("dp", "tensor", None),
        P("dp", "tensor", None),
        P("dp", "tensor", None),
        P(None, None, "tensor"),
        P("tensor", None),
        P(None, "tensor"),
        P("tensor", None),
        P(),
        P(),
        P(None, None, "tensor"),
        P("tensor", None),
        P(None, None, "tensor"),
        P("tensor", None),
        P(None, "tensor"),
        P("tensor", None),
        P(),
        P(),
    )
    return jax.shard_map(
        on_device, mesh=mesh, in_specs=in_specs, out_specs=out_specs, check_vma=False
    )
```

profile of v0, /device:TPU:0, one launch (start us, length us, event | category | flops | bytes accessed | tf_op | source)
XLA Modules:
  0.0 1815.9 jit_solution(7656307005251226870)
XLA Ops:
  21.4 8.1 all-gather.27.cloned.1.call-done
  35.8 8.3 fusion.481
  44.1 7.1 fusion.482
  57.5 8.3 fusion.483
  65.9 7.9 fusion.484
  83.8 7.8 fusion.24
  91.7 7.6 fusion.375
  105.9 9.4 fusion.27
  115.4 9.1 fusion.26
  124.6 4.5 fusion.372
  134.1 7.6 fusion.373
  146.0 9.7 multiply_convert_fusion.7
  157.7 5.6 convert_bitcast_fusion.10
  169.0 5.5 reduce-scatter.13.cloned.1.call-done
  180.0 15.0 all-gather.15.cloned.1.call-done
  204.4 8.1 fusion.486
  222.6 7.8 fusion.28
  230.4 7.5 fusion.371
  241.5 11.0 reduce-scatter.17.cloned.1.call-done
  256.6 12.0 all-gather.33.cloned.1.call-done
  268.6 9.6 multiply_convert_fusion.6
  280.2 5.6 convert_bitcast_fusion.7
  286.0 11.0 reduce-scatter.19.cloned.1.call-done
  302.7 11.9 all-gather.17.cloned.1.call-done
  314.6 10.3 fusion.77
  326.9 5.7 convert_bitcast_fusion.6
  332.9 10.8 reduce-scatter.21.cloned.1.call-done
  350.0 11.9 all-gather.19.cloned.1.call-done
  364.8 8.1 fusion.428
  372.9 8.1 fusion.427
  381.0 38.1 %fusion.367 = bf16[8,64,512]{2,1,0:T(8,128)(2,1)} fusion(bf16[1024,8,64]{0,2,1:T(8,128)(2,1)S(1)} %bitcast.631, f32[8,512,1024]{2,1,0:T(8,128)} %fusion.427, f32[8,512,1024]{2,1,0:T(8,128)} %get-tuple-element.103, f32[8,512]{1,0:T(8,128)S(1)} %log_add_fusion.5), kind=kOutput, calls=%fused_computation.364 | convolution fusion | flops 566498304 | bytes 35143680 | tf_op jit(solution)/shard_map/phqk,pkhd->pqhd/dot_general | solution.py:128
  419.1 30.6 %fusion.37 = f32[8,64,1024]{2,1,0:T(8,128)} fusion(f32[8,512,1024]{2,1,0:T(8,128)} %fusion.427, f32[8,512,1024]{2,1,0:T(8,128)} %get-tuple-element.103, f32[8,512]{1,0:T(8,128)S(1)} %log_add_fusion.5, bf16[1,1024,8,64]{1,3,2,0:T(8,128)(2,1)S(1)} %bitcast.643), kind=kOutput, calls=%fused_computation.62 | convolution fusion | flops 566236160 | bytes 69763072 | tf_op jit(solution)/shard_map/phqk,pqhd->pkhd/dot_general | solution.py:130
  449.7 7.3 fusion.92
  456.9 7.7 add_convert_fusion.7
  464.7 37.7 %fusion.364 = bf16[8,64,512]{2,1,0:T(8,128)(2,1)} fusion(bf16[1024,8,64]{0,2,1:T(8,128)(2,1)S(1)} %bitcast.632, f32[8,512,1024]{2,1,0:T(8,128)} %fusion.428, f32[8,512,1024]{2,1,0:T(8,128)} %copy-done.2, f32[8,512]{1,0:T(8,128)S(1)} %log_add_fusion.4), kind=kOutput, calls=%fused_computation.363 | convolution fusion | flops 566498304 | bytes 35143680 | tf_op jit(solution)/shard_map/phqk,pkhd->pqhd/dot_general | solution.py:128
  502.4 30.0 %add_convert_fusion.8 = bf16[8,64,1024]{2,1,0:T(8,128)(2,1)S(1)} fusion(f32[8,64,1024]{2,1,0:T(8,128)} %fusion.37, f32[8,512,1024]{2,1,0:T(8,128)} %fusion.428, f32[8,512,1024]{2,1,0:T(8,128)} %copy-done.2, f32[8,512]{1,0:T(8,128)S(1)} %log_add_fusion.4, bf16[1,1024,8,64]{1,3,2,0:T(8,128)(2,1)S(1)} %bitcast.644), kind=kOutput, calls=%fused_computation.286 | convolution fusion | flops 567284736 | bytes 70811648 | tf_op jit(solution)/shard_map/phqk,pqhd->pkhd/dot_general | solution.py:130
  542.5 11.4 reduce-scatter.23.cloned.1.call-done
  563.0 9.6 convolution_convert_fusion
  572.7 6.2 convolution_convert_fusion.1
  583.4 10.3 fusion.83
  595.7 5.7 convert_bitcast_fusion.4
  609.8 8.2 fusion.432
  618.1 37.4 %fusion.352 = bf16[8,64,512]{2,1,0:T(8,128)(2,1)} fusion(bf16[1024,8,64]{0,2,1:T(8,128)(2,1)S(1)} %bitcast.627, f32[8,512,1024]{2,1,0:T(8,128)} %fusion.432, f32[8,512,1024]{2,1,0:T(8,128)} %get-tuple-element.97, f32[8,512]{1,0:T(8,128)S(1)} %log_add_fusion), kind=kOutput, calls=%fused_computation.359 | convolution fusion | flops 566498304 | bytes 35143680 | tf_op jit(solution)/shard_map/phqk,pkhd->pqhd/dot_general | solution.py:128
  655.5 8.2 fusion.431
  663.7 37.3 %fusion.355 = bf16[8,64,512]{2,1,0:T(8,128)(2,1)} fusion(bf16[1024,8,64]{0,2,1:T(8,128)(2,1)S(1)} %bitcast.628, f32[8,512,1024]{2,1,0:T(8,128)} %fusion.431, f32[8,512,1024]{2,1,0:T(8,128)} %get-tuple-element.99, f32[8,512]{1,0:T(8,128)S(1)} %log_add_fusion.1), kind=kOutput, calls=%fused_computation.360 | convolution fusion | flops 566498304 | bytes 35143680 | tf_op jit(solution)/shard_map/phqk,pkhd->pqhd/dot_general | solution.py:128
  701.0 30.6 %fusion.61 = f32[8,64,1024]{2,1,0:T(8,128)} fusion(f32[8,512,1024]{2,1,0:T(8,128)} %fusion.431, f32[8,512,1024]{2,1,0:T(8,128)} %get-tuple-element.99, f32[8,512]{1,0:T(8,128)S(1)} %log_add_fusion.1, bf16[1,1024,8,64]{1,3,2,0:T(8,128)(2,1)S(1)} %bitcast.640), kind=kOutput, calls=%fused_computation.70 | convolution fusion | flops 566236160 | bytes 69763072 | tf_op jit(solution)/shard_map/phqk,pqhd->pkhd/dot_general | solution.py:130
  731.6 4.5 fusion.396
  736.2 8.9 fusion.84
  750.4 31.3 %add_convert_fusion.4 = bf16[8,64,1024]{2,1,0:T(8,128)(2,1)} fusion(f32[8,64,1024]{2,1,0:T(8,128)} %fusion.61, f32[8,512,1024]{2,1,0:T(8,128)} %fusion.432, f32[8,512,1024]{2,1,0:T(8,128)} %get-tuple-element.97, f32[8,512]{1,0:T(8,128)S(1)} %log_add_fusion, bf16[1,1024,8,64]{1,3,2,0:T(8,128)(2,1)} %bitcast.639), kind=kOutput, calls=%fused_computation.277 | convolution fusion | flops 567284736 | bytes 70811648 | tf_op jit(solution)/shard_map/phqk,pqhd->pkhd/dot_general | solution.py:130
  784.7 7.7 add_convert_fusion.3
  807.9 8.2 fusion.430
  816.0 8.1 fusion.429
  824.1 30.0 %fusion.358 = bf16[8,64,512]{2,1,0:T(8,128)(2,1)} fusion(bf16[1024,8,64]{0,2,1:T(8,128)(2,1)} %bitcast.623, f32[8,512,1024]{2,1,0:T(8,128)} %fusion.430, f32[8,512,1024]{2,1,0:T(8,128)} %get-tuple-element.91, f32[8,512]{1,0:T(8,128)S(1)} %copy-done.117), kind=kOutput, calls=%fused_computation.361 | convolution fusion | flops 566498304 | bytes 35143680 | tf_op jit(solution)/shard_map/phqk,pkhd->pqhd/dot_general | solution.py:128
  854.2 37.8 %fusion.361 = bf16[8,64,512]{2,1,0:T(8,128)(2,1)} fusion(bf16[1024,8,64]{0,2,1:T(8,128)(2,1)S(1)} %bitcast.624, f32[8,512,1024]{2,1,0:T(8,128)} %fusion.429, f32[8,512,1024]{2,1,0:T(8,128)} %get-tuple-element.93, f32[8,512]{1,0:T(8,128)S(1)} %copy-done.118), kind=kOutput, calls=%fused_computation.362 | convolution fusion | flops 566498304 | bytes 35143680 | tf_op jit(solution)/shard_map/phqk,pkhd->pqhd/dot_general | solution.py:128
  892.0 31.0 %fusion.49 = f32[8,64,1024]{2,1,0:T(8,128)} fusion(f32[8,512,1024]{2,1,0:T(8,128)} %fusion.429, f32[8,512,1024]{2,1,0:T(8,128)} %get-tuple-element.93, f32[8,512]{1,0:T(8,128)S(1)} %copy-done.118, bf16[1,1024,8,64]{1,3,2,0:T(8,128)(2,1)} %bitcast.635), kind=kOutput, calls=%fused_computation.66 | convolution fusion | flops 566236160 | bytes 69763072 | tf_op jit(solution)/shard_map/phqk,pqhd->pkhd/dot_general | solution.py:130
  922.9 30.8 %add_convert_fusion.6 = bf16[8,64,1024]{2,1,0:T(8,128)(2,1)} fusion(f32[8,64,1024]{2,1,0:T(8,128)} %fusion.49, f32[8,512,1024]{2,1,0:T(8,128)} %fusion.430, f32[8,512,1024]{2,1,0:T(8,128)} %get-tuple-element.91, f32[8,512]{1,0:T(8,128)S(1)} %copy-done.117, bf16[1,1024,8,64]{1,3,2,0:T(8,128)(2,1)S(1)} %bitcast.636), kind=kOutput, calls=%fused_computation.281 | convolution fusion | flops 567284736 | bytes 70811648 | tf_op jit(solution)/shard_map/phqk,pqhd->pkhd/dot_general | solution.py:130
  953.8 5.0 fusion.404
  958.8 4.7 fusion.401
  963.5 7.4 fusion.88
  975.6 6.7 fusion.261
  992.6 6.1 convolution_convert_fusion.2
  998.7 6.5 convolution_convert_fusion.3
  1031.2 46.0 %all-reduce = (f32[3,1024]{1,0:T(4,128)}, f32[3,1024]{1,0:T(4,128)}, f32[4,1024]{1,0:T(4,128)}, f32[4,1024]{1,0:T(4,128)}) all-reduce(f32[3,1024]{1,0:T(4,128)S(1)} %pad_maximum_fusion.17, f32[3,1024]{1,0:T(4,128)S(1)} %pad_maximum_fusion.18, ...), channel_id=1, replica_groups=mesh['dp'=16,'tensor'=2] {'dp','tensor'}, use_global_device_ids=true, to_apply=%region_63.64 | all-reduce | flops 14336 | bytes 114688 | tf_op jit(solution)/shard_map/psum | solution.py:342
  1080.9 693.3 %all-reduce.4.cloned.1.call-done = (bf16[3,1024,512]{2,1,0:T(8,128)(2,1)}, bf16[512,1024]{1,0:T(8,128)(2,1)}, bf16[1024,2048]{1,0:T(8,128)(2,1)}, bf16[2048,1024...) async-done(((bf16[3,1024,512]{2,1,0:T(8,128)(2,1)}, ...) | async-done | bytes 29360144 | tf_op jit(solution)/shard_map/psum | solution.py:329
  (601 shorter events, 246.2 us)
Async XLA Ops:
  7.2 231.6 %copy-start = (bf16[512,1024]{1,0:T(8,128)(2,1)S(1)}, bf16[512,1024]{1,0:T(8,128)(2,1)}, u32[]{:S(2)}) copy-start(bf16[512,1024]{1,0:T(8,128)(2,1)} %param.33) | copy-start | bytes 3145732
  7.2 22.3 %all-gather.27.cloned.1.call-start = ((), (), s32[]{:S(2)}) async-start(), calls=%async_computation.26 | async-start | bytes 3145728 | tf_op jit(solution)/shard_map/all_gather | solution.py:55
  12.0 120.5 %copy-start.101 = (f32[1,1024]{1,0:T(1,128)}, f32[1,1024]{1,0:T(1,128)S(1)}, u32[]{:S(2)}) copy-start(f32[1,1024]{1,0:T(1,128)S(1)} %get-tuple-element.84) | copy-start | bytes 12292
  16.1 35.1 %all-gather.31.cloned.1.call-start = ((), (), s32[]{:S(2)}) async-start(), calls=%async_computation.28 | async-start | bytes 3145728 | tf_op jit(solution)/shard_map/all_gather | solution.py:55
  16.4 16.5 copy-start.128
  16.8 16.0 copy-start.138
  17.4 15.4 copy-start.107
  19.5 109.6 %reduce-scatter.11.cloned.1.call-start = ((), (), s32[]{:S(2)}) async-start(), calls=%async_computation.10 | async-start | bytes 3145728 | tf_op jit(solution)/shard_map/reduce_scatter | solution.py:59
  44.1 35.8 %copy-start.85 = (f32[8,512]{1,0:T(8,128)}, f32[8,512]{1,0:T(8,128)S(1)}, u32[]{:S(2)}) copy-start(f32[8,512]{1,0:T(8,128)S(1)} %get-tuple-element.90) | copy-start | bytes 49156
  51.2 40.4 %copy-start.87 = (f32[8,512]{1,0:T(8,128)}, f32[8,512]{1,0:T(8,128)S(1)}, u32[]{:S(2)}) copy-start(f32[8,512]{1,0:T(8,128)S(1)} %get-tuple-element.92) | copy-start | bytes 49156
  57.5 16.3 slice-start
  57.5 16.3 slice-start.1
  65.9 58.6 %copy-start.89 = (f32[8,512]{1,0:T(8,128)}, f32[8,512]{1,0:T(8,128)S(1)}, u32[]{:S(2)}) copy-start(f32[8,512]{1,0:T(8,128)S(1)} %get-tuple-element.96) | copy-start | bytes 49156
  73.8 60.3 %copy-start.91 = (f32[8,512]{1,0:T(8,128)}, f32[8,512]{1,0:T(8,128)S(1)}, u32[]{:S(2)}) copy-start(f32[8,512]{1,0:T(8,128)S(1)} %get-tuple-element.98) | copy-start | bytes 49156
  83.8 15.5 copy-start.71
  102.7 43.3 %all-gather.29.cloned.1.call-start = ((), (), s32[]{:S(2)}) async-start(), calls=%async_computation.27 | async-start | bytes 3145728 | tf_op jit(solution)/shard_map/all_gather | solution.py:55
  105.9 28.2 %copy-start.20 = (bf16[1024,512]{0,1:T(8,128)(2,1)}, bf16[1024,512]{0,1:T(8,128)(2,1)S(1)}, u32[]{:S(2)}) copy-start(bf16[1024,512]{0,1:T(8,128)(2,1)S(1)} %fusion.295) | copy-start | bytes 3145732
  105.9 18.6 %slice-start.8 = ((s8[16777216]{0:T(1024)(128)(4,1)}), s8[4194304]{0:T(1024)(128)(4,1)S(1)}, s32[]{:S(2)}) async-start(s8[16777216]{0:T(1024)(128)(4,1)} %bitcast.589), calls=%async_computation.39 | async-start | bytes 8388608
  105.9 18.6 %slice-start.9 = ((s8[16777216]{0:T(1024)(128)(4,1)}), s8[4194304]{0:T(1024)(128)(4,1)S(1)}, s32[]{:S(2)}) async-start(s8[16777216]{0:T(1024)(128)(4,1)} %bitcast.589), calls=%async_computation.40 | async-start | bytes 8388608
  134.0 29.4 %reduce-scatter.15.cloned.1.call-start = ((), (), s32[]{:S(2)}) async-start(), calls=%async_computation.12 | async-start | bytes 3145728 | tf_op jit(solution)/shard_map/reduce_scatter | solution.py:59
  145.2 29.2 %reduce-scatter.13.cloned.1.call-start = ((), (), s32[]{:S(2)}) async-start(), calls=%async_computation.11 | async-start | bytes 3145728 | tf_op jit(solution)/shard_map/reduce_scatter | solution.py:59
  163.4 31.7 %all-gather.15.cloned.1.call-start = ((), (), s32[]{:S(2)}) async-start(), calls=%async_computation.13 | async-start | bytes 6291456 | tf_op jit(solution)/shard_map/all_gather | solution.py:55
  180.0 72.5 %reduce-scatter.17.cloned.1.call-start = ((), (), s32[]{:S(2)}) async-start(), calls=%async_computation.14 | async-start | bytes 3145728 | tf_op jit(solution)/shard_map/reduce_scatter | solution.py:59
  204.3 14.3 copy-start.2
  222.5 15.4 copy-start.79
  241.4 13.8 copy-start.99
  241.4 13.8 copy-start.147
  241.4 27.2 %all-gather.33.cloned.1.call-start = ((), (), s32[]{:S(2)}) async-start(), calls=%async_computation.29 | async-start | bytes 3145728 | tf_op jit(solution)/shard_map/all_gather | solution.py:55
  256.6 40.4 %reduce-scatter.19.cloned.1.call-start = ((), (), s32[]{:S(2)}) async-start(), calls=%async_computation.15 | async-start | bytes 3145728 | tf_op jit(solution)/shard_map/reduce_scatter | solution.py:59
  285.9 13.2 copy-start.100
  285.9 28.7 %all-gather.17.cloned.1.call-start = ((), (), s32[]{:S(2)}) async-start(), calls=%async_computation.16 | async-start | bytes 3145728 | tf_op jit(solution)/shard_map/all_gather | solution.py:65
  302.6 41.1 %reduce-scatter.21.cloned.1.call-start = ((), (), s32[]{:S(2)}) async-start(), calls=%async_computation.17 | async-start | bytes 3145728 | tf_op jit(solution)/shard_map/reduce_scatter | solution.py:69
  332.6 14.0 copy-start.140
  332.6 29.3 %all-gather.19.cloned.1.call-start = ((), (), s32[]{:S(2)}) async-start(), calls=%async_computation.18 | async-start | bytes 3145728 | tf_op jit(solution)/shard_map/all_gather | solution.py:65
  349.9 203.9 %reduce-scatter.23.cloned.1.call-start = ((), (), s32[]{:S(2)}) async-start(), calls=%async_computation.19 | async-start | bytes 6291456 | tf_op jit(solution)/shard_map/reduce_scatter | solution.py:69
  350.0 14.8 copy-start.23
  381.0 38.1 %copy-start.65 = (bf16[1024,512]{0,1:T(8,128)(2,1)S(1)}, bf16[1024,512]{0,1:T(8,128)(2,1)}, u32[]{:S(2)}) copy-start(bf16[1024,512]{0,1:T(8,128)(2,1)} %copy-done.64) | copy-start | bytes 3145732
  464.6 72.0 %copy-start.48 = (bf16[8,64,1024]{2,1,0:T(8,128)(2,1)}, bf16[8,64,1024]{2,1,0:T(8,128)(2,1)S(1)}, u32[]{:S(2)}) copy-start(bf16[8,64,1024]{2,1,0:T(8,128)(2,1)S(1)} %add_convert_fusion.7) | copy-start | bytes 3145732
  464.6 37.7 %copy-start.66 = (bf16[1024,512]{0,1:T(8,128)(2,1)S(1)}, bf16[1024,512]{0,1:T(8,128)(2,1)}, u32[]{:S(2)}) copy-start(bf16[1024,512]{0,1:T(8,128)(2,1)} %copy-done.64) | copy-start | bytes 3145732
  540.5 42.9 %all-gather.21.cloned.1.call-start = ((), (), s32[]{:S(2)}) async-start(), calls=%async_computation.20 | async-start | bytes 3145728 | tf_op jit(solution)/shard_map/all_gather | solution.py:65
  542.4 13.6 copy-start.5
  542.4 13.6 copy-start.10
  542.4 13.6 copy-start.94
  542.4 13.6 copy-start.97
  542.4 13.6 copy-start.104
  542.4 13.6 copy-start.120
  542.4 13.6 copy-start.125
  542.5 13.6 copy-start.135
  562.8 44.1 %all-gather.25.cloned.1.call-start = ((), (), s32[]{:S(2)}) async-start(), calls=%async_computation.24 | async-start | bytes 3145728 | tf_op jit(solution)/shard_map/all_gather | solution.py:65
  582.9 162.2 %reduce-scatter.25.cloned.1.call-start = ((), (), s32[]{:S(2)}) async-start(), calls=%async_computation.21 | async-start | bytes 3145728 | tf_op jit(solution)/shard_map/reduce_scatter | solution.py:69
  583.4 12.3 copy-start.154
  601.4 203.1 %all-gather.23.cloned.1.call-start = ((), (), s32[]{:S(2)}) async-start(), calls=%async_computation.22 | async-start | bytes 3145728 | tf_op jit(solution)/shard_map/all_gather | solution.py:65
  609.8 126.4 %copy-start.35 = (bf16[1024,512]{0,1:T(8,128)(2,1)}, bf16[1024,512]{0,1:T(8,128)(2,1)S(1)}, u32[]{:S(2)}) copy-start(bf16[1024,512]{0,1:T(8,128)(2,1)S(1)} %fusion.325) | copy-start | bytes 3145732
  663.7 37.3 %copy-start.63 = (bf16[1024,512]{0,1:T(8,128)(2,1)S(1)}, bf16[1024,512]{0,1:T(8,128)(2,1)}, u32[]{:S(2)}) copy-start(bf16[1024,512]{0,1:T(8,128)(2,1)} %copy-done.62) | copy-start | bytes 3145732
  701.0 30.6 %copy-start.176 = (bf16[8,64,512]{2,1,0:T(8,128)(2,1)S(1)}, bf16[8,64,512]{2,1,0:T(8,128)(2,1)}, u32[]{:S(2)}) copy-start(bf16[8,64,512]{2,1,0:T(8,128)(2,1)} %fusion.352) | copy-start | bytes 1572868
  701.0 30.6 %copy-start.177 = (bf16[8,64,512]{2,1,0:T(8,128)(2,1)S(1)}, bf16[8,64,512]{2,1,0:T(8,128)(2,1)}, u32[]{:S(2)}) copy-start(bf16[8,64,512]{2,1,0:T(8,128)(2,1)} %fusion.355) | copy-start | bytes 1572868
  750.3 270.0 %reduce-scatter.29.cloned.1.call-start = ((), (), s32[]{:S(2)}) async-start(), calls=%async_computation.25 | async-start | bytes 3145728 | tf_op jit(solution)/shard_map/reduce_scatter | solution.py:69
  797.4 230.0 %reduce-scatter.27.cloned.1.call-start = ((), (), s32[]{:S(2)}) async-start(), calls=%async_computation.23 | async-start | bytes 3145728 | tf_op jit(solution)/shard_map/reduce_scatter | solution.py:69
  824.1 30.0 %copy-start.51 = (bf16[1024,512]{0,1:T(8,128)(2,1)S(1)}, bf16[1024,512]{0,1:T(8,128)(2,1)}, u32[]{:S(2)}) copy-start(bf16[1024,512]{0,1:T(8,128)(2,1)} %copy-done.50) | copy-start | bytes 3145732
  824.1 30.0 %copy-start.118 = (f32[8,512]{1,0:T(8,128)S(1)}, f32[8,512]{1,0:T(8,128)}, u32[]{:S(2)}) copy-start(f32[8,512]{1,0:T(8,128)} %log_add_fusion.3) | copy-start | bytes 49156
  892.0 31.0 %copy-start.61 = (bf16[1024,512]{0,1:T(8,128)(2,1)S(1)}, bf16[1024,512]{0,1:T(8,128)(2,1)}, u32[]{:S(2)}) copy-start(bf16[1024,512]{0,1:T(8,128)(2,1)} %copy-done.60) | copy-start | bytes 3145732
  953.8 17.2 slice-start.4
  982.3 791.9 %all-reduce.4.cloned.1.call-start = ((), (), s32[]{:S(2)}) async-start(), calls=%async_computation.30 | async-start | bytes 58720256 | tf_op jit(solution)/shard_map/psum | solution.py:329
  1027.4 49.8 %copy-start.30 = (bf16[1,1,512,1024]{3,2,1,0:T(8,128)(2,1)S(1)}, bf16[1,1,512,1024]{3,2,1,0:T(8,128)(2,1)}, u32[]{:S(2)}) copy-start(bf16[1,1,512,1024]{3,2,1,0:T(8,128)(2,1)} %reduce-scatter.27.cloned.1.call-done) | copy-start | bytes 3145732
  (160 other events, 774.0 us)
Sparse Core Ops, SparseCore 0:
  16.2 13.2 all-gather.26
  31.6 11.7 all-gather.30
  102.8 10.9 reduce-scatter.10
  134.2 11.8 all-gather.28
  148.7 10.9 reduce-scatter.14
  163.5 10.9 reduce-scatter.12
  180.1 14.9 all-gather.14
  241.5 10.8 reduce-scatter.16
  256.7 11.8 all-gather.32
  286.0 10.9 reduce-scatter.18
  302.7 11.8 all-gather.16
  332.8 10.9 reduce-scatter.20
  350.0 11.8 all-gather.18
  540.6 13.2 reduce-scatter.22
  562.9 11.8 all-gather.20
  583.0 11.8 all-gather.24
  601.6 11.0 reduce-scatter.24
  750.4 11.8 all-gather.22
  797.5 11.0 reduce-scatter.28
  982.4 11.0 reduce-scatter.26
  1014.7 759.4 all-reduce.3
where the time goes:
time: 1820 us
  waiting for transfers between devices  803 us (44%)
  matrix products  763 us (42%)
  other arithmetic  157 us (9%)
  blocking collectives  46 us (3%)
  local copies, waits for them, and re-layouts  26 us (1%)
  between operations  18.3 us (1%)
    psum x1, waiting for transfers between devices, on_device(): lax.psum(enc_grads[0].astype(jnp.bfloat16), 'dp').astype(jnp.float32)  693 us
    dot_general x6, matrix products, attend_backward(): jnp.einsum('phqk,pkhd->pqhd', grad_scores, keys, preferred_element_type=j...  218 us
    dot_general x6, matrix products, attend_backward(): jnp.einsum('phqk,pqhd->pkhd', grad_scores, query_block, preferred_element...  184 us
    dot_general x16, matrix products, back_project(): jnp.einsum('psh,dh->psd', grad, weight, preferred_element_type=jnp.float32)  74.6 us
    dot_general x16, matrix products, project(): jnp.einsum('psd,dh->psh', left, weight, preferred_element_type=jnp.float32)  64.4 us
    dot_general x16, matrix products, weight_grad(): jnp.einsum('psd,psh->dh', left, grad, preferred_element_type=jnp.float32)  52.8 us
    dot_general x6, matrix products, attend_backward(): jnp.einsum('pqhd,pkhd->phqk', grad_block, values, preferred_element_type=...  48.9 us
    psum x1, blocking collectives, on_device(): lax.psum((jnp.stack([gain_a1, gain_a2, gain_mem]), jnp.stack([bias_a1, bi...  46 us
  transfers between devices with their start and end apart: 21, of which 12 were waited for; matrix products, arithmetic and copies ran while one was open for 30% of the time, Pallas kernels for 0%

commit v1 on v0

v1 whole, which is shorter than its diff:
```python
import math
from functools import partial

import jax
import jax.numpy as jnp
from jax import lax
from jax.experimental import pallas as pl
from jax.experimental.pallas import tpu as pltpu
from jax.sharding import PartitionSpec as P

HEAD_DIM = 64
PAIR = 2 * HEAD_DIM
QBLK = 512
QBLK_BACK = 512
BF = jnp.bfloat16
F32 = jnp.float32

epsilon = 1e-05
root_half = 1.0 / math.sqrt(2.0)
root_two_pi = 1.0 / math.sqrt(2.0 * math.pi)
score_scale = HEAD_DIM**-0.5
log2_scale = score_scale * math.log2(math.e)
NEG = -1e30


def norm_forward(hidden, gain, shift):
    center = hidden - jnp.mean(hidden, axis=-1, keepdims=True)
    inverse = lax.rsqrt(jnp.mean(center * center, axis=-1, keepdims=True) + epsilon)
    normed = center * inverse
    return (normed * gain + shift, normed, inverse)


def norm_backward(grad, normed, inverse, gain):
    scaled = grad * gain
    inner = (
        scaled
        - jnp.mean(scaled, axis=-1, keepdims=True)
        - normed * jnp.mean(scaled * normed, axis=-1, keepdims=True)
    )
    return (inverse * inner, jnp.sum(grad * normed, axis=0), jnp.sum(grad, axis=0))


def gelu_value(zed):
    return 0.5 * zed * (1.0 + lax.erf(zed * root_half))


def gelu_slope(zed):
    return 0.5 * (1.0 + lax.erf(zed * root_half)) + zed * jnp.exp(-0.5 * zed * zed) * root_two_pi


def dot(left, right, left_dim, right_dim):
    return lax.dot_general(
        left, right, (((left_dim,), (right_dim,)), ((), ())), preferred_element_type=F32
    )


def project(left, weight):
    return dot(left, weight, 1, 0)


def back_project(grad, weight):
    return dot(grad, weight, 1, 1)


def weight_grad(left, grad):
    return dot(left, grad, 0, 0)


def swap(value):
    return lax.ppermute(value, "tensor", [(0, 1), (1, 0)])


def spread(rows):
    if lax.axis_size("tensor") == 2:
        return jnp.concatenate([rows, swap(rows)], axis=0)
    return lax.all_gather(rows, "tensor", axis=0, tiled=True)


def collect(partial_rows):
    if lax.axis_size("tensor") == 2:
        half = partial_rows.shape[0] // 2
        return partial_rows[:half] + swap(partial_rows[half:].astype(BF)).astype(F32)
    return lax.psum_scatter(
        partial_rows.astype(BF), "tensor", scatter_dimension=0, tiled=True
    ).astype(F32)


def lane_of(shape):
    return lax.broadcasted_iota(jnp.int32, shape, 1)


def head_lanes(value, head, spare):
    lane = lane_of(value.shape)
    mine = (lane >= head * HEAD_DIM) & (lane < (head + 1) * HEAD_DIM)
    slot = lane == (1 - head) * HEAD_DIM
    return jnp.where(mine, value, jnp.where(slot, spare, 0.0)).astype(BF)


def positions(count, axis, shape, start, shift, total):
    pos = lax.broadcasted_iota(jnp.int32, shape, axis) + (start + shift)
    return jnp.where(pos >= total, pos - total, pos)


def masked_keys(meta_ref, k_ref, kh_ref):
    total = k_ref.shape[0]
    keys = k_ref[...].astype(F32)
    pos = positions(total, 0, keys.shape, 0, meta_ref[0], total)
    spare = jnp.where(pos < meta_ref[1], 0.0, NEG)
    for head in range(2):
        kh_ref[head] = head_lanes(keys, head, spare)


def scores_of(meta_ref, kh_ref, head, query_f32, start, causal):
    total = kh_ref.shape[1]
    scores = dot(kh_ref[head], head_lanes(query_f32, head, 1.0), 1, 1)
    if causal:
        shape = scores.shape
        key_pos = positions(total, 0, (total, 1), 0, meta_ref[0], total)
        query_pos = positions(shape[1], 1, (1, shape[1]), start, meta_ref[0], total)
        scores = jnp.where(key_pos <= query_pos, scores, NEG)
    return scores


def forward_kernel(meta_ref, q_ref, k_ref, v_ref, ctx_ref, lse_ref, kh_ref, vt_ref, *, causal):
    block = pl.program_id(1)

    @pl.when(block == 0)
    def _():
        masked_keys(meta_ref, k_ref, kh_ref)
        vt_ref[...] = v_ref[...].astype(F32).T.astype(BF)

    query = q_ref[...].astype(F32)
    start = block * q_ref.shape[0]
    parts = []
    for head in range(2):
        scores = scores_of(meta_ref, kh_ref, head, query, start, causal)
        top = jnp.max(scores, axis=0, keepdims=True) * log2_scale
        weights = jnp.exp2(scores * log2_scale - top)
        total = jnp.sum(weights, axis=0, keepdims=True)
        values = vt_ref[head * HEAD_DIM : (head + 1) * HEAD_DIM, :]
        parts.append(dot(values, weights.astype(BF), 1, 0) / total)
        lse_ref[0, head : head + 1, :] = top + jnp.log2(total)
    ctx_ref[...] = jnp.concatenate(parts, axis=0).T.astype(BF)


def backward_kernel(
    meta_ref,
    q_ref,
    k_ref,
    v_ref,
    do_ref,
    ctx_ref,
    lse_ref,
    dq_ref,
    dk_ref,
    dv_ref,
    kh_ref,
    kt_ref,
    dk_acc,
    dv_acc,
    *,
    causal,
):
    block = pl.program_id(1)

    @pl.when(block == 0)
    def _():
        masked_keys(meta_ref, k_ref, kh_ref)
        kt_ref[...] = k_ref[...].astype(F32).T.astype(BF)
        dk_acc[...] = jnp.zeros_like(dk_acc)
        dv_acc[...] = jnp.zeros_like(dv_acc)

    query = q_ref[...].astype(F32)
    grad = do_ref[...].astype(F32)
    start = block * q_ref.shape[0]
    products = (grad * ctx_ref[...].astype(F32)).T
    parts = []
    for head in range(2):
        low, high = head * HEAD_DIM, (head + 1) * HEAD_DIM
        scores = scores_of(meta_ref, kh_ref, head, query, start, causal)
        soft = jnp.exp2(scores * log2_scale - lse_ref[0, head : head + 1, :])
        grad_head = head_lanes(grad, head, 0.0)
        row_dot = jnp.sum(products[low:high, :], axis=0, keepdims=True)
        grad_soft = dot(v_ref[...], grad_head, 1, 1)
        grad_scores = (soft * (grad_soft - row_dot)).astype(BF)
        dv_acc[...] += dot(soft.astype(BF), grad_head, 1, 0)
        dk_acc[...] += dot(grad_scores, head_lanes(query, head, 0.0), 1, 0)
        parts.append(dot(kt_ref[low:high, :], grad_scores, 1, 0))
    dq_ref[...] = (jnp.concatenate(parts, axis=0).T * score_scale).astype(BF)

    @pl.when(block == pl.num_programs(1) - 1)
    def _():
        dk_ref[...] = (dk_acc[...] * score_scale).astype(BF)
        dv_ref[...] = dv_acc[...].astype(BF)


def row_spec(rows):
    return pl.BlockSpec((rows, PAIR), lambda pair, block, meta: (block, pair))


def whole_spec(rows):
    return pl.BlockSpec((rows, PAIR), lambda pair, block, meta: (0, pair))


def lse_spec(rows):
    return pl.BlockSpec((1, 2, rows), lambda pair, block, meta: (pair, 0, block))


def attend_forward(meta, queries, keys, values, causal):
    total, width = queries.shape
    pairs = width // PAIR
    rows = min(QBLK, total)
    return pl.pallas_call(
        partial(forward_kernel, causal=causal),
        grid_spec=pltpu.PrefetchScalarGridSpec(
            num_scalar_prefetch=1,
            grid=(pairs, total // rows),
            in_specs=[row_spec(rows), whole_spec(total), whole_spec(total)],
            out_specs=[row_spec(rows), lse_spec(rows)],
            scratch_shapes=[pltpu.VMEM((2, total, PAIR), BF), pltpu.VMEM((PAIR, total), BF)],
        ),
        out_shape=[
            jax.ShapeDtypeStruct((total, width), BF),
            jax.ShapeDtypeStruct((pairs, 2, total), F32),
        ],
        name="attend_forward",
    )(meta, queries, keys, values)


def attend_backward(meta, queries, keys, values, grad, context, log_sums, causal):
    total, width = queries.shape
    pairs = width // PAIR
    rows = min(QBLK_BACK, total)
    return pl.pallas_call(
        partial(backward_kernel, causal=causal),
        grid_spec=pltpu.PrefetchScalarGridSpec(
            num_scalar_prefetch=1,
            grid=(pairs, total // rows),
            in_specs=[
                row_spec(rows),
                whole_spec(total),
                whole_spec(total),
                row_spec(rows),
                row_spec(rows),
                lse_spec(rows),
            ],
            out_specs=[row_spec(rows), whole_spec(total), whole_spec(total)],
            scratch_shapes=[
                pltpu.VMEM((2, total, PAIR), BF),
                pltpu.VMEM((PAIR, total), BF),
                pltpu.VMEM((total, PAIR), F32),
                pltpu.VMEM((total, PAIR), F32),
            ],
        ),
        out_shape=[jax.ShapeDtypeStruct((total, width), BF)] * 3,
        name="attend_backward",
    )(meta, queries, keys, values, grad, context, log_sums)


def attention_forward(query_in, memory_in, w_qkv, w_out, meta, causal):
    queries = project(query_in, w_qkv[0]).astype(BF)
    keys = project(memory_in, w_qkv[1]).astype(BF)
    values = project(memory_in, w_qkv[2]).astype(BF)
    context, log_sums = attend_forward(meta, queries, keys, values, causal)
    return (collect(project(context, w_out)), (queries, keys, values, context, log_sums))


def attention_backward(grad_out, query_in, memory_in, w_qkv, w_out, kept, meta, causal):
    queries, keys, values, context, log_sums = kept
    grad_full = spread(grad_out.astype(BF))
    grad_context = back_project(grad_full, w_out).astype(BF)
    grad_w_out = weight_grad(grad_full, context).astype(BF)
    grad_q, grad_k, grad_v = attend_backward(
        meta, queries, keys, values, grad_context, context, log_sums, causal
    )
    first = jnp.concatenate(
        [weight_grad(query_in, grad_q).astype(BF), weight_grad(memory_in, grad_k).astype(BF)]
    )
    second = jnp.concatenate([weight_grad(memory_in, grad_v).astype(BF), grad_w_out])
    from_query = back_project(grad_q, w_qkv[0])
    from_memory = back_project(grad_k, w_qkv[1]) + back_project(grad_v, w_qkv[2])
    return ((first, second), from_query, from_memory)


def ffn_forward(normed_rows, w_in, w_out):
    rows_full = spread(normed_rows)
    zed = project(rows_full, w_in)
    unit = gelu_value(zed).astype(BF)
    result = collect(project(unit, w_out))
    return (result, (rows_full, zed, unit, w_in, w_out))


def ffn_backward(grad_out, kept):
    rows, zed, unit, w_in, w_out = kept
    grad_full = spread(grad_out.astype(BF))
    grad_w_out = weight_grad(unit, grad_full).astype(BF)
    grad_unit = back_project(grad_full, w_out).astype(BF)
    grad_zed = (grad_unit.astype(F32) * gelu_slope(zed)).astype(BF)
    grad_w_in = weight_grad(rows, grad_zed).astype(BF)
    grad_input = collect(back_project(grad_zed, w_in))
    return (grad_input, (grad_w_in, grad_w_out))


def copy_out_kernel(index_ref, src_ref, keep_ref, send_ref):
    step = pl.program_id(0)
    half = pl.num_programs(0) // 2

    @pl.when(step < half)
    def _():
        keep_ref[...] = src_ref[...]

    @pl.when(step >= half)
    def _():
        send_ref[...] = src_ref[...]


def copy_in_kernel(index_ref, near_ref, far_ref, out_ref):
    step = pl.program_id(0)
    half = pl.num_programs(0) // 2

    @pl.when(step < half)
    def _():
        out_ref[...] = near_ref[...].astype(F32)

    @pl.when(step >= half)
    def _():
        out_ref[...] = far_ref[...].astype(F32)


def chunk_specs(count, rows, cols):
    half = count // 2
    block = (1, rows, cols)
    whole = pl.BlockSpec(block, lambda step, index: (step ^ index[0], 0, 0))
    near = pl.BlockSpec(block, lambda step, index: (jnp.minimum(step, half - 1), 0, 0))
    far = pl.BlockSpec(block, lambda step, index: (jnp.maximum(step - half, 0), 0, 0))
    return (whole, near, far)


def partner(value, bit):
    count = lax.axis_size("dp")
    return lax.ppermute(value, "dp", [(at, at ^ (1 << bit)) for at in range(count)])


def sum_over_pairs(value, first_bits):
    count = lax.axis_size("dp")
    levels = count.bit_length() - 1
    order = list(first_bits) + [bit for bit in range(levels) if bit not in first_bits]
    place = lax.axis_index("dp")
    index = jnp.zeros((), jnp.int32)
    for bit in order:
        index = index * 2 + ((place >> bit) & 1)
    index = index[None]
    rows = value.shape[0] // count
    cols = value.shape[1]
    half = count // 2
    whole, near, far = chunk_specs(count, rows, cols)
    keep, send = pl.pallas_call(
        copy_out_kernel,
        grid_spec=pltpu.PrefetchScalarGridSpec(
            num_scalar_prefetch=1, grid=(count,), in_specs=[whole], out_specs=[near, far]
        ),
        out_shape=[jax.ShapeDtypeStruct((half, rows, cols), BF)] * 2,
        name="copy_out",
    )(index, value.reshape(count, rows, cols))
    for level, bit in enumerate(order):
        summed = keep + partner(send, bit)
        if level + 1 < levels:
            middle = summed.shape[0] // 2
            keep, send = summed[:middle], summed[middle:]
    for bit in order[:0:-1]:
        summed = jnp.concatenate([summed, partner(summed, bit)])
    other = partner(summed, order[0])
    result = pl.pallas_call(
        copy_in_kernel,
        grid_spec=pltpu.PrefetchScalarGridSpec(
            num_scalar_prefetch=1, grid=(count,), in_specs=[near, far], out_specs=whole
        ),
        out_shape=jax.ShapeDtypeStruct((count, rows, cols), F32),
        name="copy_in",
    )(index, summed, other)
    return result.reshape(value.shape)


def sum_two(pair):
    return (sum_over_pairs(pair[0], (0, 1)), sum_over_pairs(pair[1], (1, 0)))


def sum_everywhere(value):
    for axis in ("tensor", "dp"):
        count = lax.axis_size(axis)
        for bit in range(count.bit_length() - 1):
            value = value + lax.ppermute(
                value, axis, [(at, at ^ (1 << bit)) for at in range(count)]
            )
    return value


def split_attention(pair):
    first, second = pair
    rows = first.shape[0] // 2
    return (
        jnp.concatenate([first, second[:rows]]).reshape(3, rows, first.shape[1]),
        second[rows:].T,
    )


def on_device(
    src,
    tgt,
    src_len,
    tgt_len,
    enc_qkv,
    enc_out_w,
    enc_ffn_in,
    enc_ffn_out,
    enc_gain,
    enc_bias,
    dec_qkv,
    dec_self_out,
    dec_cross,
    dec_cross_out,
    dec_ffn_in,
    dec_ffn_out,
    dec_gain,
    dec_bias,
    enc_cot,
    dec_cot,
):
    if lax.axis_size("tensor") == 2:
        shift = (lax.axis_index("tensor") * src.shape[1]).astype(jnp.int32)
    else:
        shift = jnp.zeros((), jnp.int32)
    src_meta = jnp.stack([shift, src_len[0]])
    tgt_meta = jnp.stack([shift, tgt_len[0]])
    source = src[0].astype(F32)
    target = tgt[0].astype(F32)
    ln_a1, nm_a1, inv_a1 = norm_forward(source, enc_gain[0], enc_bias[0])
    ln_b1, nm_b1, inv_b1 = norm_forward(target, dec_gain[0], dec_bias[0])
    enc_rows = spread(ln_a1.astype(BF))
    dec_rows = spread(ln_b1.astype(BF))
    attn_enc, keep_enc_attn = attention_forward(
        enc_rows, enc_rows, enc_qkv, enc_out_w, src_meta, False
    )
    hidden_one = source + attn_enc
    ln_a2, nm_a2, inv_a2 = norm_forward(hidden_one, enc_gain[1], enc_bias[1])
    ffn_enc, keep_enc_ffn = ffn_forward(ln_a2.astype(BF), enc_ffn_in, enc_ffn_out)
    hidden_two = hidden_one + ffn_enc
    ln_mem, nm_mem, inv_mem = norm_forward(hidden_two, enc_gain[2], enc_bias[2])
    memory = ln_mem.astype(BF)
    attn_self, keep_self = attention_forward(
        dec_rows, dec_rows, dec_qkv, dec_self_out, tgt_meta, True
    )
    resid_one = target + attn_self
    ln_b2, nm_b2, inv_b2 = norm_forward(resid_one, dec_gain[1], dec_bias[1])
    cross_rows = spread(ln_b2.astype(BF))
    memory_rows = spread(memory)
    attn_cross, keep_cross = attention_forward(
        cross_rows, memory_rows, dec_cross, dec_cross_out, src_meta, False
    )
    resid_two = resid_one + attn_cross
    ln_b3, nm_b3, inv_b3 = norm_forward(resid_two, dec_gain[2], dec_bias[2])
    ffn_dec, keep_dec_ffn = ffn_forward(ln_b3.astype(BF), dec_ffn_in, dec_ffn_out)
    resid_three = resid_two + ffn_dec
    ln_final, nm_final, inv_final = norm_forward(resid_three, dec_gain[3], dec_bias[3])
    grad_r3, gain_final, bias_final = norm_backward(
        dec_cot[0].astype(F32), nm_final, inv_final, dec_gain[3]
    )
    grad_b3, dec_ffn_grads = ffn_backward(grad_r3, keep_dec_ffn)
    dec_ffn_sums = sum_two(dec_ffn_grads)
    part_r2, gain_b3, bias_b3 = norm_backward(grad_b3, nm_b3, inv_b3, dec_gain[2])
    grad_r2 = grad_r3 + part_r2
    cross_grads, from_query, from_memory = attention_backward(
        grad_r2,
        cross_rows,
        memory_rows,
        dec_cross,
        dec_cross_out,
        keep_cross,
        src_meta,
        False,
    )
    cross_sums = split_attention(sum_two(cross_grads))
    grad_memory = enc_cot[0].astype(F32) + collect(from_memory)
    grad_h2, gain_mem, bias_mem = norm_backward(grad_memory, nm_mem, inv_mem, enc_gain[2])
    grad_a2, enc_ffn_grads = ffn_backward(grad_h2, keep_enc_ffn)
    enc_ffn_sums = sum_two(enc_ffn_grads)
    part_r1, gain_b2, bias_b2 = norm_backward(collect(from_query), nm_b2, inv_b2, dec_gain[1])
    grad_r1 = grad_r2 + part_r1
    self_grads, self_query, self_memory = attention_backward(
        grad_r1, dec_rows, dec_rows, dec_qkv, dec_self_out, keep_self, tgt_meta, True
    )
    self_sums = split_attention(sum_two(self_grads))
    grad_b1 = collect(self_query + self_memory)
    part_tgt, gain_b1, bias_b1 = norm_backward(grad_b1, nm_b1, inv_b1, dec_gain[0])
    grad_tgt = grad_r1 + part_tgt
    part_h1, gain_a2, bias_a2 = norm_backward(grad_a2, nm_a2, inv_a2, enc_gain[1])
    grad_h1 = grad_h2 + part_h1
    enc_grads, enc_query, enc_memory = attention_backward(
        grad_h1, enc_rows, enc_rows, enc_qkv, enc_out_w, keep_enc_attn, src_meta, False
    )
    enc_sums = split_attention(sum_two(enc_grads))
    grad_a1 = collect(enc_query + enc_memory)
    part_src, gain_a1, bias_a1 = norm_backward(grad_a1, nm_a1, inv_a1, enc_gain[0])
    grad_src = grad_h1 + part_src
    small = sum_everywhere(
        jnp.stack(
            [
                gain_a1,
                gain_a2,
                gain_mem,
                bias_a1,
                bias_a2,
                bias_mem,
                gain_b1,
                gain_b2,
                gain_b3,
                gain_final,
                bias_b1,
                bias_b2,
                bias_b3,
                bias_final,
            ]
        )
    )
    return (
        memory[None],
        ln_final.astype(BF)[None],
        grad_src[None],
        grad_tgt[None],
        enc_sums[0],
        enc_sums[1],
        enc_ffn_sums[0],
        enc_ffn_sums[1],
        small[0:3],
        small[3:6],
        self_sums[0],
        self_sums[1],
        cross_sums[0],
        cross_sums[1],
        dec_ffn_sums[0],
        dec_ffn_sums[1],
        small[6:10],
        small[10:14],
    )


def solution(mesh):
    rows = P("dp", "tensor", None)
    triple = P(None, None, "tensor")
    in_specs = (
        rows,
        rows,
        P("dp"),
        P("dp"),
        triple,
        P("tensor", None),
        P(None, "tensor"),
        P("tensor", None),
        P(),
        P(),
        triple,
        P("tensor", None),
        triple,
        P("tensor", None),
        P(None, "tensor"),
        P("tensor", None),
        P(),
        P(),
        rows,
        rows,
    )
    out_specs = (
        rows,
        rows,
        rows,
        rows,
        triple,
        P("tensor", None),
        P(None, "tensor"),
        P("tensor", None),
        P(),
        P(),
        triple,
        P("tensor", None),
        triple,
        P("tensor", None),
        P(None, "tensor"),
        P("tensor", None),
        P(),
        P(),
    )
    return jax.shard_map(
        on_device, mesh=mesh, in_specs=in_specs, out_specs=out_specs, check_vma=False
    )
```

time: 1820 us -> 1190 us (0.65); the launches traced: 1820 us -> 1160 us
  matrix products: 763 us -> 194 us
  waiting for transfers between devices: 803 us -> 310 us
  Pallas kernels: 0 us -> 351 us
  starting transfers between devices: 2.11 us -> 108 us
  blocking collectives: 46 us -> 0 us
  local copies, waits for them, and re-layouts: 26 us -> 61.3 us
  other arithmetic: 157 us -> 135 us
    psum x1 -> x0, waiting for transfers between devices: 693 us -> none  [on_device(): lax.psum(enc_grads[0].astype(jnp.bfloat16), 'dp').astype(jnp.float32)]
    dot_general x84 -> x48, matrix products: 763 us -> 194 us  [dot(): lax.dot_general(left, right, (((left_dim,), (right_dim,)), ((), ())), pre...]
    pallas_call x0 -> x26, Pallas kernels: none -> 351 us  [the longest x10 104 us: sum_over_pairs(): pl.pallas_call(copy_in_kernel, grid_spec=pltpu.PrefetchScalarGridSpec(num...]
    ppermute x0 -> x107, waiting for transfers between devices: none -> 310 us  [the longest x80 286 us: partner(): lax.ppermute(value, 'dp', [(at, at ^ 1 << bit) for at in range(count)])]
    ppermute x0 -> x107, starting transfers between devices: none -> 108 us  [the longest x80 98 us: partner(): lax.ppermute(value, 'dp', [(at, at ^ 1 << bit) for at in range(count)])]
    all_gather x10 -> x0, waiting for transfers between devices: 59.7 us -> none  [the longest x5 35.8 us: spread(): return lax.all_gather(stacked, 'tensor', axis=2, tiled=True)]
    concatenate x3 -> x39, other arithmetic: 0.35 us -> 56.7 us  [the longest x30 30.5 us: sum_over_pairs(): summed = jnp.concatenate([summed, partner(summed, bit)])]
    reduce_scatter x10 -> x0, waiting for transfers between devices: 49.7 us -> none  [the longest x5 27.5 us: collect(): lax.psum_scatter(partial_rows.astype(jnp.bfloat16), 'tensor', scatter_dim...]
  transfers between devices with their start and end apart: 21 -> 107, of which waited for: 12 -> 37; matrix products, arithmetic and copies ran while one was open for 30% -> 27% of each run, Pallas kernels for 0% -> 27%
where the time goes in v1:
time: 1190 us; the launch traced here: 1160 us
  Pallas kernels  351 us (29%)
  waiting for transfers between devices  310 us (26%)
  matrix products  194 us (16%)
  other arithmetic  135 us (11%)
  starting transfers between devices  108 us (9%)
  local copies, waits for them, and re-layouts  61.3 us (5%)
    ppermute x80, waiting for transfers between devices, partner(): lax.ppermute(value, 'dp', [(at, at ^ 1 << bit) for at in range(count)])  286 us
    dot_general x48, matrix products, dot(): lax.dot_general(left, right, (((left_dim,), (right_dim,)), ((), ())), pre...  194 us
    pallas_call x10, Pallas kernels, sum_over_pairs(): pl.pallas_call(copy_in_kernel, grid_spec=pltpu.PrefetchScalarGridSpec(num...  104 us
    pallas_call x10, Pallas kernels, sum_over_pairs(): pl.pallas_call(copy_out_kernel, grid_spec=pltpu.PrefetchScalarGridSpec(nu...  98.8 us
    ppermute x80, starting transfers between devices, partner(): lax.ppermute(value, 'dp', [(at, at ^ 1 << bit) for at in range(count)])  98 us
    pallas_call x3, Pallas kernels, attend_backward(): pl.pallas_call(partial(backward_kernel, causal=causal), grid_spec=pltpu.P...  85.7 us
    pallas_call x3, Pallas kernels, attend_forward(): pl.pallas_call(partial(forward_kernel, causal=causal), grid_spec=pltpu.Pr...  62.9 us
    concatenate x30, other arithmetic, sum_over_pairs(): summed = jnp.concatenate([summed, partner(summed, bit)])  30.5 us
  transfers between devices with their start and end apart: 107, of which 37 were waited for; matrix products, arithmetic and copies ran while one was open for 27% of the time, Pallas kernels for 27%

profile of v1, /device:TPU:0, one launch (start us, length us, event | category | flops | bytes accessed | tf_op | source)
XLA Modules:
  0.0 1164.4 jit_solution(14324493396547918275)
XLA Ops:
  20.9 21.0 %attend_forward.3 = (bf16[1024,512]{1,0:T(8,128)(2,1)}, f32[4,2,1024]{2,1,0:T(2,128)}) custom-call(s32[2]{0:T(128)} %pad_add_fusion.meta_ref, bf16[1024,512]{1,0:T(8,128)(2,1)} %convolution_convert_fusion.27.q_ref, bf16[1024,512]{1,0:T(8,128)(2,1)} %convolution_convert_fusion.26.k_ref, bf16[1024,512]{1,0:T(8,128)(2,1)} %convolution_convert_fusion.25.v_ref), custom_call_target="tpu_custom_call" | custom-call | tf_op jit(solution)/shard_map/attend_forward/pallas_call | solution.py:213
  59.9 20.6 %attend_forward.4 = (bf16[1024,512]{1,0:T(8,128)(2,1)}, f32[4,2,1024]{2,1,0:T(2,128)}) custom-call(s32[2]{0:T(128)} %pad_add_fusion.1.meta_ref, bf16[1024,512]{1,0:T(8,128)(2,1)} %convolution_convert_fusion.24.q_ref, bf16[1024,512]{1,0:T(8,128)(2,1)} %convolution_convert_fusion.23.k_ref, bf16[1024,512]{1,0:T(8,128)(2,1)} %convolution_convert_fusion.22.v_ref), custom_call_target="tpu_custom_call" | custom-call | tf_op jit(solution)/shard_map/attend_forward/pallas_call | solution.py:213
  83.8 8.8 multiply_convert_fusion.1
  110.9 21.3 %attend_forward.5 = (bf16[1024,512]{1,0:T(8,128)(2,1)}, f32[4,2,1024]{2,1,0:T(2,128)}) custom-call(s32[2]{0:T(128)} %pad_add_fusion.meta_ref, bf16[1024,512]{1,0:T(8,128)(2,1)} %convolution_convert_fusion.21.q_ref, bf16[1024,512]{1,0:T(8,128)(2,1)} %convolution_convert_fusion.20.k_ref, bf16[1024,512]{1,0:T(8,128)(2,1)} %convolution_convert_fusion.19.v_ref), custom_call_target="tpu_custom_call" | custom-call | tf_op jit(solution)/shard_map/attend_forward/pallas_call | solution.py:213
  142.3 7.2 multiply_convert_fusion
  171.0 8.7 fusion.5
  179.8 6.3 fusion.155
  201.2 6.0 convolution_convert_fusion.1
  207.2 10.4 copy_out.18
  220.6 9.4 convolution_convert_fusion
  230.0 10.2 copy_out.19
  245.5 28.1 %attend_backward.3 = (bf16[1024,512]{1,0:T(8,128)(2,1)}, bf16[1024,512]{1,0:T(8,128)(2,1)}, bf16[1024,512]{1,0:T(8,128)(2,1)}) custom-call(s32[2]{0:T(128)} %pad_add_fusion.meta_ref, bf16[1024,512]{1,0:T(8,128)(2,1)} %convolution_convert_fusion.21.q_ref, bf16[1024,512]{1,0:T(8,128)(2,1)} %convolution_convert_fusion.20.k_ref, ...), custom_call_target="tpu_custom_call" | custom-call | tf_op jit(solution)/shard_map/attend_backward/pallas_call | solution.py:234
  279.3 9.6 copy_out.16
  294.9 9.6 copy_out.17
  346.1 7.1 collective-permute-done.92
  358.6 5.9 collective-permute-done.84
  366.8 4.9 collective-permute-done.93
  373.3 12.4 %collective-permute-done.101 = bf16[2,128,1024]{2,1,0:T(8,128)(2,1)S(1)} collective-permute-done((bf16[2,128,1024]{2,1,0:T(8,128)(2,1)S(1)}, bf16[2,128,1024]{2,1,0:T(8,128)(2,1)S(1)}, u32[]{:S(2)}, u32[]{:S(2)}) %collective-permute-start.101) | collective-permute-done | bytes 524320 | tf_op jit(solution)/shard_map/ppermute | solution.py:341
  387.5 7.0 collective-permute-done.85
  398.3 10.6 collective-permute-done.94
  409.0 12.1 %collective-permute-done.86 = bf16[1,128,512]{2,1,0:T(8,128)(2,1)S(1)} collective-permute-done((bf16[1,128,512]{2,1,0:T(8,128)(2,1)S(1)}, bf16[1,128,512]{2,1,0:T(8,128)(2,1)S(1)}, u32[]{:S(2)}, u32[]{:S(2)}) %collective-permute-start.86) | collective-permute-done | bytes 131104 | tf_op jit(solution)/shard_map/ppermute | solution.py:341
  428.4 9.0 collective-permute-done.87
  440.2 11.2 collective-permute-start.88
  452.2 11.2 fusion.11
  463.3 6.7 fusion.156
  474.4 29.6 %attend_backward.5 = (bf16[1024,512]{1,0:T(8,128)(2,1)}, bf16[1024,512]{1,0:T(8,128)(2,1)}, bf16[1024,512]{1,0:T(8,128)(2,1)}) custom-call(s32[2]{0:T(128)} %pad_add_fusion.1.meta_ref, bf16[1024,512]{1,0:T(8,128)(2,1)} %convolution_convert_fusion.24.q_ref, bf16[1024,512]{1,0:T(8,128)(2,1)} %convolution_convert_fusion.23.k_ref, ...), custom_call_target="tpu_custom_call" | custom-call | tf_op jit(solution)/shard_map/attend_backward/pallas_call | solution.py:234
  503.9 4.9 fusion.72
  513.6 6.3 convolution_convert_fusion.2
  519.8 8.1 convolution_convert_fusion.3
  542.4 9.5 copy_out.14
  551.9 9.5 copy_out.15
  567.5 7.1 add_add_fusion
  574.6 10.2 copy_out.13
  584.8 10.4 copy_out.12
  603.7 5.7 collective-permute-done.81
  628.8 59.6 %collective-permute-done.68 = bf16[4,128,512]{2,1,0:T(8,128)(2,1)} collective-permute-done((bf16[4,128,512]{2,1,0:T(8,128)(2,1)}, bf16[4,128,512]{2,1,0:T(8,128)(2,1)}, u32[]{:S(2)}, u32[]{:S(2)}) %collective-permute-start.68) | collective-permute-done | bytes 524320 | tf_op jit(solution)/shard_map/ppermute | solution.py:341
  703.1 11.5 collective-permute-done.90.far_ref
  716.2 9.9 copy_in.17
  734.1 10.0 copy_in.16
  747.2 6.2 pad_maximum_fusion.2
  772.5 28.0 %attend_backward.4 = (bf16[1024,512]{1,0:T(8,128)(2,1)}, bf16[1024,512]{1,0:T(8,128)(2,1)}, bf16[1024,512]{1,0:T(8,128)(2,1)}) custom-call(s32[2]{0:T(128)} %pad_add_fusion.meta_ref, bf16[1024,512]{1,0:T(8,128)(2,1)} %convolution_convert_fusion.27.q_ref, bf16[1024,512]{1,0:T(8,128)(2,1)} %convolution_convert_fusion.26.k_ref, ...), custom_call_target="tpu_custom_call" | custom-call | tf_op jit(solution)/shard_map/attend_backward/pallas_call | solution.py:234
  824.8 9.5 copy_out.10
  834.4 9.8 copy_out.11
  862.7 10.1 collective-permute-done.55
  873.8 6.2 collective-permute-done.65
  900.3 7.8 collective-permute-done.41
  908.3 8.4 collective-permute-done.49
  920.1 24.6 %collective-permute-done.33 = bf16[1,128,512]{2,1,0:T(8,128)(2,1)S(1)} collective-permute-done((bf16[1,128,512]{2,1,0:T(8,128)(2,1)S(1)}, bf16[1,128,512]{2,1,0:T(8,128)(2,1)S(1)}, u32[]{:S(2)}, u32[]{:S(2)}) %collective-permute-start.33) | collective-permute-done | bytes 131104 | tf_op jit(solution)/shard_map/ppermute | solution.py:341
  948.9 6.1 collective-permute-start.43
  959.3 23.1 %collective-permute-done.35 = bf16[2,128,512]{2,1,0:T(8,128)(2,1)S(1)} collective-permute-done((bf16[2,128,512]{2,1,0:T(8,128)(2,1)S(1)}, bf16[2,128,512]{2,1,0:T(8,128)(2,1)S(1)}, u32[]{:S(2)}, u32[]{:S(2)}) %collective-permute-start.35) | collective-permute-done | bytes 262176 | tf_op jit(solution)/shard_map/ppermute | solution.py:341
  993.4 23.7 %collective-permute-done.36 = bf16[4,128,512]{2,1,0:T(8,128)(2,1)S(1)} collective-permute-done((bf16[4,128,512]{2,1,0:T(8,128)(2,1)S(1)}, bf16[4,128,512]{2,1,0:T(8,128)(2,1)S(1)}, u32[]{:S(2)}, u32[]{:S(2)}) %collective-permute-start.36) | collective-permute-done | bytes 524320 | tf_op jit(solution)/shard_map/ppermute | solution.py:341
  1022.0 6.5 collective-permute-done.44
  1030.6 8.9 collective-permute-done.52
  1044.7 6.3 collective-permute-done.74.far_ref
  1053.4 11.0 copy_in.19
  1064.4 11.0 copy_in.18
  1075.3 10.0 copy_in.15
  1094.7 10.1 copy_in.14
  1104.9 5.6 pad_maximum_fusion.1
  1110.5 9.9 copy_in.11
  1126.4 10.1 copy_in.10
  1136.5 5.6 pad_maximum_fusion
  1142.1 11.0 copy_in.13
  1153.1 11.1 copy_in.12
  (769 shorter events, 411.5 us)
Async XLA Ops:
  7.6 38.8 %collective-permute-start.4 = (bf16[512,1024]{0,1:T(8,128)(2,1)S(1)}, bf16[512,1024]{0,1:T(8,128)(2,1)}, u32[]{:S(2)}, u32[]{:S(2)}) collective-permute-start(bf16[512,1024]{0,1:T(8,128)(2,1)S(1)} %fusion.34), channel_id=1, source_target_pairs={{0,1},{1,0},{2,3},{3,2},{4,5},{5,4},{6,7},{7,6},{8,9},{9,8},{10,11... | collective-permute-start | bytes 3145736 | tf_op jit(solution)/shard_map/ppermute | solution.py:70
  52.3 31.5 %collective-permute-start.2 = (bf16[512,1024]{1,0:T(8,128)(2,1)}, bf16[512,1024]{1,0:T(8,128)(2,1)}, u32[]{:S(2)}, u32[]{:S(2)}) collective-permute-start(bf16[512,1024]{1,0:T(8,128)(2,1)} %add_convert_fusion.4), channel_id=1, source_target_pairs={{0,1},{1,0},{2,3},{3,2},{4,5},{5,4},{6,7},{7,6},{8,9},{9,8},{10,11... | collective-permute-start | bytes 3145736 | tf_op jit(solution)/shard_map/ppermute | solution.py:70
  201.0 40.6 %collective-permute-start.13 = (bf16[512,1024]{0,1:T(8,128)(2,1)}, bf16[512,1024]{0,1:T(8,128)(2,1)}, u32[]{:S(2)}, u32[]{:S(2)}) collective-permute-start(bf16[512,1024]{0,1:T(8,128)(2,1)} %get-tuple-element.140), channel_id=1, source_target_pairs={{0,1},{1,0},{2,3},{3,2},{4,5},{5,4},{6,7},{7,6},{8,9},{9,8},{10,11... | collective-permute-start | bytes 3145736 | tf_op jit(solution)/shard_map/ppermute | solution.py:70
  217.6 102.7 %collective-permute-start.91 = (bf16[8,64,2048]{2,1,0:T(8,128)(2,1)}, bf16[8,64,2048]{2,1,0:T(8,128)(2,1)}, u32[]{:S(2)}, u32[]{:S(2)}) collective-permute-start(bf16[8,64,2048]{2,1,0:T(8,128)(2,1)} %get-tuple-element.85), channel_id=1, source_target_pairs={{0,2},{2,0},{4,6},{6,4},{8,10},{10,8},{12,14},{14,12},{16,18},{18,... | collective-permute-start | bytes 6291464 | tf_op jit(solution)/shard_map/ppermute | solution.py:341
  240.2 84.0 %collective-permute-start.99 = (bf16[8,128,1024]{2,1,0:T(8,128)(2,1)}, bf16[8,128,1024]{2,1,0:T(8,128)(2,1)}, u32[]{:S(2)}, u32[]{:S(2)}) collective-permute-start(bf16[8,128,1024]{2,1,0:T(8,128)(2,1)} %get-tuple-element.87), channel_id=1, source_target_pairs={{0,4},{2,6},{4,0},{6,2},{8,12},{10,14},{12,8},{14,10},{16,20},{18,... | collective-permute-start | bytes 6291464 | tf_op jit(solution)/shard_map/ppermute | solution.py:341
  304.5 26.3 %collective-permute-start.83 = (bf16[8,128,512]{2,1,0:T(8,128)(2,1)}, bf16[8,128,512]{2,1,0:T(8,128)(2,1)}, u32[]{:S(2)}, u32[]{:S(2)}) collective-permute-start(bf16[8,128,512]{2,1,0:T(8,128)(2,1)} %get-tuple-element.83), channel_id=1, source_target_pairs={{0,4},{2,6},{4,0},{6,2},{8,12},{10,14},{12,8},{14,10},{16,20},{18,... | collective-permute-start | bytes 3145736 | tf_op jit(solution)/shard_map/ppermute | solution.py:341
  305.0 28.1 %collective-permute-start.75 = (bf16[8,128,512]{2,1,0:T(8,128)(2,1)}, bf16[8,128,512]{2,1,0:T(8,128)(2,1)}, u32[]{:S(2)}, u32[]{:S(2)}) collective-permute-start(bf16[8,128,512]{2,1,0:T(8,128)(2,1)} %get-tuple-element.81), channel_id=1, source_target_pairs={{0,2},{2,0},{4,6},{6,4},{8,10},{10,8},{12,14},{14,12},{16,18},{18,... | collective-permute-start | bytes 3145736 | tf_op jit(solution)/shard_map/ppermute | solution.py:341
  324.2 29.0 %collective-permute-start.92 = (bf16[4,64,2048]{2,1,0:T(8,128)(2,1)S(1)}, bf16[4,64,2048]{2,1,0:T(8,128)(2,1)S(1)}, u32[]{:S(2)}, u32[]{:S(2)}) collective-permute-start(bf16[4,64,2048]{2,1,0:T(8,128)(2,1)S(1)} %slice.590), channel_id=1, source_target_pairs={{0,4},{2,6},{4,0},{6,2},{8,12},{10,14},{12,8},{14,10},{16,20},{18,... | collective-permute-start | bytes 3145736 | tf_op jit(solution)/shard_map/ppermute | solution.py:341
  333.1 31.3 %collective-permute-start.84 = (bf16[4,128,512]{2,1,0:T(8,128)(2,1)S(1)}, bf16[4,128,512]{2,1,0:T(8,128)(2,1)S(1)}, u32[]{:S(2)}, u32[]{:S(2)}) collective-permute-start(bf16[4,128,512]{2,1,0:T(8,128)(2,1)S(1)} %slice.582), channel_id=1, source_target_pairs={{0,2},{2,0},{4,6},{6,4},{8,10},{10,8},{12,14},{14,12},{16,18},{18,... | collective-permute-start | bytes 1572872 | tf_op jit(solution)/shard_map/ppermute | solution.py:341
  336.4 29.7 %collective-permute-start.76 = (bf16[4,128,512]{2,1,0:T(8,128)(2,1)S(1)}, bf16[4,128,512]{2,1,0:T(8,128)(2,1)S(1)}, u32[]{:S(2)}, u32[]{:S(2)}) collective-permute-start(bf16[4,128,512]{2,1,0:T(8,128)(2,1)S(1)} %slice.576), channel_id=1, source_target_pairs={{0,4},{2,6},{4,0},{6,2},{8,12},{10,14},{12,8},{14,10},{16,20},{18,... | collective-permute-start | bytes 1572872 | tf_op jit(solution)/shard_map/ppermute | solution.py:341
  342.0 110.1 %collective-permute-start.15 = (bf16[512,1024]{1,0:T(8,128)(2,1)S(1)}, bf16[512,1024]{1,0:T(8,128)(2,1)S(1)}, u32[]{:S(2)}, u32[]{:S(2)}) collective-permute-start(bf16[512,1024]{1,0:T(8,128)(2,1)S(1)} %get-tuple-element.137), channel_id=1, source_target_pairs={{0,1},{1,0},{2,3},{3,2},{4,5},{5,4},{6,7},{7,6},{8,9},{9,8},{10,11... | collective-permute-start | bytes 3145736 | tf_op jit(solution)/shard_map/ppermute | solution.py:70
  353.2 118.0 %collective-permute-start.20 = (bf16[512,1024]{0,1:T(8,128)(2,1)S(1)}, bf16[512,1024]{0,1:T(8,128)(2,1)S(1)}, u32[]{:S(2)}, u32[]{:S(2)}) collective-permute-start(bf16[512,1024]{0,1:T(8,128)(2,1)S(1)} %get-tuple-element.133), channel_id=1, source_target_pairs={{0,1},{1,0},{2,3},{3,2},{4,5},{5,4},{6,7},{7,6},{8,9},{9,8},{10,11... | collective-permute-start | bytes 3145736 | tf_op jit(solution)/shard_map/ppermute | solution.py:70
  366.2 28.3 %collective-permute-start.85 = (bf16[2,128,512]{2,1,0:T(8,128)(2,1)S(1)}, bf16[2,128,512]{2,1,0:T(8,128)(2,1)S(1)}, u32[]{:S(2)}, u32[]{:S(2)}) collective-permute-start(bf16[2,128,512]{2,1,0:T(8,128)(2,1)S(1)} %slice.584), channel_id=1, source_target_pairs={{0,8},{2,10},{4,12},{6,14},{8,0},{10,2},{12,4},{14,6},{16,24},{18,... | collective-permute-start | bytes 786440 | tf_op jit(solution)/shard_map/ppermute | solution.py:341
  371.7 26.6 %collective-permute-start.77 = (bf16[2,128,512]{2,1,0:T(8,128)(2,1)S(1)}, bf16[2,128,512]{2,1,0:T(8,128)(2,1)S(1)}, u32[]{:S(2)}, u32[]{:S(2)}) collective-permute-start(bf16[2,128,512]{2,1,0:T(8,128)(2,1)S(1)} %slice.578), channel_id=1, source_target_pairs={{0,8},{2,10},{4,12},{6,14},{8,0},{10,2},{12,4},{14,6},{16,24},{18,... | collective-permute-start | bytes 786440 | tf_op jit(solution)/shard_map/ppermute | solution.py:341
  394.5 30.9 %collective-permute-start.102 = (bf16[1,128,1024]{2,1,0:T(8,128)(2,1)S(1)}, bf16[1,128,1024]{2,1,0:T(8,128)(2,1)S(1)}, u32[]{:S(2)}, u32[]{:S(2)}) collective-permute-start(bf16[1,128,1024]{2,1,0:T(8,128)(2,1)S(1)} %slice.600), channel_id=1, source_target_pairs={{0,16},{2,18},{4,20},{6,22},{8,24},{10,26},{12,28},{14,30},{16,0},... | collective-permute-start | bytes 786440 | tf_op jit(solution)/shard_map/ppermute | solution.py:341
  421.1 117.2 %collective-permute-start.95 = (bf16[1,64,2048]{2,1,0:T(8,128)(2,1)S(1)}, bf16[1,64,2048]{2,1,0:T(8,128)(2,1)S(1)}, u32[]{:S(2)}, u32[]{:S(2)}) collective-permute-start(bf16[1,64,2048]{2,1,0:T(8,128)(2,1)S(1)} %slice_add_fusion.26), channel_id=1, source_target_pairs={{0,16},{2,18},{4,20},{6,22},{8,24},{10,26},{12,28},{14,30},{16,0},... | collective-permute-start | bytes 786440 | tf_op jit(solution)/shard_map/ppermute | solution.py:341
  437.4 124.0 %collective-permute-start.103 = (bf16[1,128,1024]{2,1,0:T(8,128)(2,1)S(1)}, bf16[1,128,1024]{2,1,0:T(8,128)(2,1)S(1)}, u32[]{:S(2)}, u32[]{:S(2)}) collective-permute-start(bf16[1,128,1024]{2,1,0:T(8,128)(2,1)S(1)} %slice_add_fusion.25), channel_id=1, source_target_pairs={{0,16},{2,18},{4,20},{6,22},{8,24},{10,26},{12,28},{14,30},{16,0},... | collective-permute-start | bytes 786440 | tf_op jit(solution)/shard_map/ppermute | solution.py:341
  440.2 123.2 %collective-permute-start.88 = (bf16[2,128,512]{2,1,0:T(8,128)(2,1)}, bf16[2,128,512]{2,1,0:T(8,128)(2,1)}, u32[]{:S(2)}, u32[]{:S(2)}) collective-permute-start(bf16[2,128,512]{2,1,0:T(8,128)(2,1)} %pad_maximum_fusion.65), channel_id=1, source_target_pairs={{0,8},{2,10},{4,12},{6,14},{8,0},{10,2},{12,4},{14,6},{16,24},{18,... | collective-permute-start | bytes 786440 | tf_op jit(solution)/shard_map/ppermute | solution.py:341
  452.1 113.1 %collective-permute-start.80 = (bf16[2,128,512]{2,1,0:T(8,128)(2,1)}, bf16[2,128,512]{2,1,0:T(8,128)(2,1)S(1)}, u32[]{:S(2)}, u32[]{:S(2)}) collective-permute-start(bf16[2,128,512]{2,1,0:T(8,128)(2,1)} %pad_maximum_fusion.64), channel_id=1, source_target_pairs={{0,8},{2,10},{4,12},{6,14},{8,0},{10,2},{12,4},{14,6},{16,24},{18,... | collective-permute-start | bytes 786440 | tf_op jit(solution)/shard_map/ppermute | solution.py:341
  471.2 147.4 %collective-permute-start.16 = (bf16[512,1024]{1,0:T(8,128)(2,1)}, bf16[512,1024]{1,0:T(8,128)(2,1)S(1)}, u32[]{:S(2)}, u32[]{:S(2)}) collective-permute-start(bf16[512,1024]{1,0:T(8,128)(2,1)} %slice.792), channel_id=1, source_target_pairs={{0,1},{1,0},{2,3},{3,2},{4,5},{5,4},{6,7},{7,6},{8,9},{9,8},{10,11... | collective-permute-start | bytes 3145736 | tf_op jit(solution)/shard_map/ppermute | solution.py:70
  539.2 26.3 %collective-permute-start.96 = (bf16[2,64,2048]{2,1,0:T(8,128)(2,1)}, bf16[2,64,2048]{2,1,0:T(8,128)(2,1)S(1)}, u32[]{:S(2)}, u32[]{:S(2)}) collective-permute-start(bf16[2,64,2048]{2,1,0:T(8,128)(2,1)} %pad_maximum_fusion.58), channel_id=1, source_target_pairs={{0,8},{2,10},{4,12},{6,14},{8,0},{10,2},{12,4},{14,6},{16,24},{18,... | collective-permute-start | bytes 1572872 | tf_op jit(solution)/shard_map/ppermute | solution.py:341
  561.4 49.4 %collective-permute-start.67 = (bf16[8,128,512]{2,1,0:T(8,128)(2,1)}, bf16[8,128,512]{2,1,0:T(8,128)(2,1)}, u32[]{:S(2)}, u32[]{:S(2)}) collective-permute-start(bf16[8,128,512]{2,1,0:T(8,128)(2,1)} %get-tuple-element.79), channel_id=1, source_target_pairs={{0,4},{2,6},{4,0},{6,2},{8,12},{10,14},{12,8},{14,10},{16,20},{18,... | collective-permute-start | bytes 3145736 | tf_op jit(solution)/shard_map/ppermute | solution.py:341
  563.4 51.0 %collective-permute-start.59 = (bf16[8,128,512]{2,1,0:T(8,128)(2,1)}, bf16[8,128,512]{2,1,0:T(8,128)(2,1)}, u32[]{:S(2)}, u32[]{:S(2)}) collective-permute-start(bf16[8,128,512]{2,1,0:T(8,128)(2,1)} %get-tuple-element.77), channel_id=1, source_target_pairs={{0,2},{2,0},{4,6},{6,4},{8,10},{10,8},{12,14},{14,12},{16,18},{18,... | collective-permute-start | bytes 3145736 | tf_op jit(solution)/shard_map/ppermute | solution.py:341
  565.2 31.8 %collective-permute-start.104 = (bf16[2,128,1024]{2,1,0:T(8,128)(2,1)}, bf16[2,128,1024]{2,1,0:T(8,128)(2,1)}, u32[]{:S(2)}, u32[]{:S(2)}) collective-permute-start(bf16[2,128,1024]{2,1,0:T(8,128)(2,1)} %pad_maximum_fusion.59), channel_id=1, source_target_pairs={{0,8},{2,10},{4,12},{6,14},{8,0},{10,2},{12,4},{14,6},{16,24},{18,... | collective-permute-start | bytes 1572872 | tf_op jit(solution)/shard_map/ppermute | solution.py:341
  565.5 35.9 %collective-permute-start.89 = (bf16[4,128,512]{2,1,0:T(8,128)(2,1)}, bf16[4,128,512]{2,1,0:T(8,128)(2,1)}, u32[]{:S(2)}, u32[]{:S(2)}) collective-permute-start(bf16[4,128,512]{2,1,0:T(8,128)(2,1)} %pad_maximum_fusion.57), channel_id=1, source_target_pairs={{0,2},{2,0},{4,6},{6,4},{8,10},{10,8},{12,14},{14,12},{16,18},{18,... | collective-permute-start | bytes 1572872 | tf_op jit(solution)/shard_map/ppermute | solution.py:341
  609.3 146.4 %collective-permute-start.38 = (bf16[8,64,2048]{2,1,0:T(8,128)(2,1)}, bf16[8,64,2048]{2,1,0:T(8,128)(2,1)}, u32[]{:S(2)}, u32[]{:S(2)}) collective-permute-start(bf16[8,64,2048]{2,1,0:T(8,128)(2,1)} %get-tuple-element.73), channel_id=1, source_target_pairs={{0,2},{2,0},{4,6},{6,4},{8,10},{10,8},{12,14},{14,12},{16,18},{18,... | collective-permute-start | bytes 6291464 | tf_op jit(solution)/shard_map/ppermute | solution.py:341
  610.8 83.5 %collective-permute-start.97 = (bf16[4,64,2048]{2,1,0:T(8,128)(2,1)}, bf16[4,64,2048]{2,1,0:T(8,128)(2,1)}, u32[]{:S(2)}, u32[]{:S(2)}) collective-permute-start(bf16[4,64,2048]{2,1,0:T(8,128)(2,1)} %pad_maximum_fusion.48), channel_id=1, source_target_pairs={{0,4},{2,6},{4,0},{6,2},{8,12},{10,14},{12,8},{14,10},{16,20},{18,... | collective-permute-start | bytes 3145736 | tf_op jit(solution)/shard_map/ppermute | solution.py:341
  614.4 84.3 %collective-permute-start.105 = (bf16[4,128,1024]{2,1,0:T(8,128)(2,1)}, bf16[4,128,1024]{2,1,0:T(8,128)(2,1)}, u32[]{:S(2)}, u32[]{:S(2)}) collective-permute-start(bf16[4,128,1024]{2,1,0:T(8,128)(2,1)} %pad_maximum_fusion.49), channel_id=1, source_target_pairs={{0,2},{2,0},{4,6},{6,4},{8,10},{10,8},{12,14},{14,12},{16,18},{18,... | collective-permute-start | bytes 3145736 | tf_op jit(solution)/shard_map/ppermute | solution.py:341
  618.7 69.7 %collective-permute-start.68 = (bf16[4,128,512]{2,1,0:T(8,128)(2,1)}, bf16[4,128,512]{2,1,0:T(8,128)(2,1)}, u32[]{:S(2)}, u32[]{:S(2)}) collective-permute-start(bf16[4,128,512]{2,1,0:T(8,128)(2,1)} %slice.568), channel_id=1, source_target_pairs={{0,2},{2,0},{4,6},{6,4},{8,10},{10,8},{12,14},{14,12},{16,18},{18,... | collective-permute-start | bytes 1572872 | tf_op jit(solution)/shard_map/ppermute | solution.py:341
  620.8 69.7 %collective-permute-start.60 = (bf16[4,128,512]{2,1,0:T(8,128)(2,1)}, bf16[4,128,512]{2,1,0:T(8,128)(2,1)}, u32[]{:S(2)}, u32[]{:S(2)}) collective-permute-start(bf16[4,128,512]{2,1,0:T(8,128)(2,1)} %slice.562), channel_id=1, source_target_pairs={{0,4},{2,6},{4,0},{6,2},{8,12},{10,14},{12,8},{14,10},{16,20},{18,... | collective-permute-start | bytes 1572872 | tf_op jit(solution)/shard_map/ppermute | solution.py:341
  688.4 26.2 %collective-permute-start.90 = (bf16[8,128,512]{2,1,0:T(8,128)(2,1)}, bf16[8,128,512]{2,1,0:T(8,128)(2,1)S(1)}, u32[]{:S(2)}, u32[]{:S(2)}) collective-permute-start(bf16[8,128,512]{2,1,0:T(8,128)(2,1)} %pad_maximum_fusion.47.near_ref), channel_id=1, source_target_pairs={{0,4},{2,6},{4,0},{6,2},{8,12},{10,14},{12,8},{14,10},{16,20},{18,... | collective-permute-start | bytes 3145736 | tf_op jit(solution)/shard_map/ppermute | solution.py:341
  690.5 70.3 %collective-permute-start.46 = (bf16[8,128,1024]{2,1,0:T(8,128)(2,1)}, bf16[8,128,1024]{2,1,0:T(8,128)(2,1)}, u32[]{:S(2)}, u32[]{:S(2)}) collective-permute-start(bf16[8,128,1024]{2,1,0:T(8,128)(2,1)} %get-tuple-element.75), channel_id=1, source_target_pairs={{0,4},{2,6},{4,0},{6,2},{8,12},{10,14},{12,8},{14,10},{16,20},{18,... | collective-permute-start | bytes 6291464 | tf_op jit(solution)/shard_map/ppermute | solution.py:341
  698.7 34.0 %collective-permute-start.82 = (bf16[8,128,512]{2,1,0:T(8,128)(2,1)S(1)}, bf16[8,128,512]{2,1,0:T(8,128)(2,1)}, u32[]{:S(2)}, u32[]{:S(2)}) collective-permute-start(bf16[8,128,512]{2,1,0:T(8,128)(2,1)S(1)} %copy-done.44), channel_id=1, source_target_pairs={{0,2},{2,0},{4,6},{6,4},{8,10},{10,8},{12,14},{14,12},{16,18},{18,... | collective-permute-start | bytes 3145736 | tf_op jit(solution)/shard_map/ppermute | solution.py:341
  702.4 66.4 %collective-permute-start.17 = (bf16[512,1024]{1,0:T(8,128)(2,1)}, bf16[512,1024]{1,0:T(8,128)(2,1)}, u32[]{:S(2)}, u32[]{:S(2)}) collective-permute-start(bf16[512,1024]{1,0:T(8,128)(2,1)} %get-tuple-element.135), channel_id=1, source_target_pairs={{0,1},{1,0},{2,3},{3,2},{4,5},{5,4},{6,7},{7,6},{8,9},{9,8},{10,11... | collective-permute-start | bytes 3145736 | tf_op jit(solution)/shard_map/ppermute | solution.py:70
  759.8 95.5 %collective-permute-start.39 = (bf16[4,64,2048]{2,1,0:T(8,128)(2,1)}, bf16[4,64,2048]{2,1,0:T(8,128)(2,1)}, u32[]{:S(2)}, u32[]{:S(2)}) collective-permute-start(bf16[4,64,2048]{2,1,0:T(8,128)(2,1)} %slice.548), channel_id=1, source_target_pairs={{0,4},{2,6},{4,0},{6,2},{8,12},{10,14},{12,8},{14,10},{16,20},{18,... | collective-permute-start | bytes 3145736 | tf_op jit(solution)/shard_map/ppermute | solution.py:341
  765.1 94.3 %collective-permute-start.47 = (bf16[4,128,1024]{2,1,0:T(8,128)(2,1)}, bf16[4,128,1024]{2,1,0:T(8,128)(2,1)}, u32[]{:S(2)}, u32[]{:S(2)}) collective-permute-start(bf16[4,128,1024]{2,1,0:T(8,128)(2,1)} %slice.554), channel_id=1, source_target_pairs={{0,2},{2,0},{4,6},{6,4},{8,10},{10,8},{12,14},{14,12},{16,18},{18,... | collective-permute-start | bytes 3145736 | tf_op jit(solution)/shard_map/ppermute | solution.py:341
  765.9 55.3 %collective-permute-start.72 = (bf16[2,128,512]{2,1,0:T(8,128)(2,1)S(1)}, bf16[2,128,512]{2,1,0:T(8,128)(2,1)S(1)}, u32[]{:S(2)}, u32[]{:S(2)}) collective-permute-start(bf16[2,128,512]{2,1,0:T(8,128)(2,1)S(1)} %pad_maximum_fusion.63), channel_id=1, source_target_pairs={{0,8},{2,10},{4,12},{6,14},{8,0},{10,2},{12,4},{14,6},{16,24},{18,... | collective-permute-start | bytes 786440 | tf_op jit(solution)/shard_map/ppermute | solution.py:341
  767.8 76.4 %collective-permute-start.64 = (bf16[2,128,512]{2,1,0:T(8,128)(2,1)}, bf16[2,128,512]{2,1,0:T(8,128)(2,1)}, u32[]{:S(2)}, u32[]{:S(2)}) collective-permute-start(bf16[2,128,512]{2,1,0:T(8,128)(2,1)} %pad_maximum_fusion.62), channel_id=1, source_target_pairs={{0,8},{2,10},{4,12},{6,14},{8,0},{10,2},{12,4},{14,6},{16,24},{18,... | collective-permute-start | bytes 786440 | tf_op jit(solution)/shard_map/ppermute | solution.py:341
  807.4 39.7 %collective-permute-start.18 = (bf16[512,1024]{1,0:T(8,128)(2,1)}, bf16[512,1024]{1,0:T(8,128)(2,1)}, u32[]{:S(2)}, u32[]{:S(2)}) collective-permute-start(bf16[512,1024]{1,0:T(8,128)(2,1)} %slice.791), channel_id=1, source_target_pairs={{0,1},{1,0},{2,3},{3,2},{4,5},{5,4},{6,7},{7,6},{8,9},{9,8},{10,11... | collective-permute-start | bytes 3145736 | tf_op jit(solution)/shard_map/ppermute | solution.py:70
  822.1 31.8 %collective-permute-start.73 = (bf16[4,128,512]{2,1,0:T(8,128)(2,1)}, bf16[4,128,512]{2,1,0:T(8,128)(2,1)}, u32[]{:S(2)}, u32[]{:S(2)}) collective-permute-start(bf16[4,128,512]{2,1,0:T(8,128)(2,1)} %pad_maximum_fusion.55), channel_id=1, source_target_pairs={{0,2},{2,0},{4,6},{6,4},{8,10},{10,8},{12,14},{14,12},{16,18},{18,... | collective-permute-start | bytes 1572872 | tf_op jit(solution)/shard_map/ppermute | solution.py:341
  844.2 38.9 %collective-permute-start.30 = (bf16[8,128,512]{2,1,0:T(8,128)(2,1)}, bf16[8,128,512]{2,1,0:T(8,128)(2,1)}, u32[]{:S(2)}, u32[]{:S(2)}) collective-permute-start(bf16[8,128,512]{2,1,0:T(8,128)(2,1)} %get-tuple-element.71), channel_id=1, source_target_pairs={{0,4},{2,6},{4,0},{6,2},{8,12},{10,14},{12,8},{14,10},{16,20},{18,... | collective-permute-start | bytes 3145736 | tf_op jit(solution)/shard_map/ppermute | solution.py:341
  847.1 38.3 %collective-permute-start.22 = (bf16[8,128,512]{2,1,0:T(8,128)(2,1)}, bf16[8,128,512]{2,1,0:T(8,128)(2,1)}, u32[]{:S(2)}, u32[]{:S(2)}) collective-permute-start(bf16[8,128,512]{2,1,0:T(8,128)(2,1)} %get-tuple-element.69), channel_id=1, source_target_pairs={{0,2},{2,0},{4,6},{6,4},{8,10},{10,8},{12,14},{14,12},{16,18},{18,... | collective-permute-start | bytes 3145736 | tf_op jit(solution)/shard_map/ppermute | solution.py:341
  853.9 26.2 %collective-permute-start.65 = (bf16[4,128,512]{2,1,0:T(8,128)(2,1)}, bf16[4,128,512]{2,1,0:T(8,128)(2,1)S(1)}, u32[]{:S(2)}, u32[]{:S(2)}) collective-permute-start(bf16[4,128,512]{2,1,0:T(8,128)(2,1)} %pad_maximum_fusion.54), channel_id=1, source_target_pairs={{0,4},{2,6},{4,0},{6,2},{8,12},{10,14},{12,8},{14,10},{16,20},{18,... | collective-permute-start | bytes 1572872 | tf_op jit(solution)/shard_map/ppermute | solution.py:341
  857.0 32.6 %collective-permute-start.40 = (bf16[2,64,2048]{2,1,0:T(8,128)(2,1)S(1)}, bf16[2,64,2048]{2,1,0:T(8,128)(2,1)S(1)}, u32[]{:S(2)}, u32[]{:S(2)}) collective-permute-start(bf16[2,64,2048]{2,1,0:T(8,128)(2,1)S(1)} %slice.550), channel_id=1, source_target_pairs={{0,8},{2,10},{4,12},{6,14},{8,0},{10,2},{12,4},{14,6},{16,24},{18,... | collective-permute-start | bytes 1572872 | tf_op jit(solution)/shard_map/ppermute | solution.py:341
  888.3 69.0 %collective-permute-start.57 = (f32[14,1024]{1,0:T(8,128)S(1)}, f32[14,1024]{1,0:T(8,128)S(1)}, u32[]{:S(2)}, u32[]{:S(2)}) collective-permute-start(f32[14,1024]{1,0:T(8,128)S(1)} %add.481), channel_id=1, source_target_pairs={{0,8},{2,10},{4,12},{6,14},{8,0},{10,2},{12,4},{14,6},{16,24},{18,... | collective-permute-start | bytes 172040 | tf_op jit(solution)/shard_map/ppermute | solution.py:392
  908.2 40.6 %collective-permute-start.42 = (bf16[1,64,2048]{2,1,0:T(8,128)(2,1)S(1)}, bf16[1,64,2048]{2,1,0:T(8,128)(2,1)S(1)}, u32[]{:S(2)}, u32[]{:S(2)}) collective-permute-start(bf16[1,64,2048]{2,1,0:T(8,128)(2,1)S(1)} %slice_add_fusion.32), channel_id=1, source_target_pairs={{0,16},{2,18},{4,20},{6,22},{8,24},{10,26},{12,28},{14,30},{16,0},... | collective-permute-start | bytes 786440 | tf_op jit(solution)/shard_map/ppermute | solution.py:341
  916.8 38.2 %collective-permute-start.50 = (bf16[1,128,1024]{2,1,0:T(8,128)(2,1)S(1)}, bf16[1,128,1024]{2,1,0:T(8,128)(2,1)S(1)}, u32[]{:S(2)}, u32[]{:S(2)}) collective-permute-start(bf16[1,128,1024]{2,1,0:T(8,128)(2,1)S(1)} %slice_add_fusion.31), channel_id=1, source_target_pairs={{0,16},{2,18},{4,20},{6,22},{8,24},{10,26},{12,28},{14,30},{16,0},... | collective-permute-start | bytes 786440 | tf_op jit(solution)/shard_map/ppermute | solution.py:341
  916.9 27.7 %collective-permute-start.33 = (bf16[1,128,512]{2,1,0:T(8,128)(2,1)S(1)}, bf16[1,128,512]{2,1,0:T(8,128)(2,1)S(1)}, u32[]{:S(2)}, u32[]{:S(2)}) collective-permute-start(bf16[1,128,512]{2,1,0:T(8,128)(2,1)S(1)} %slice.544), channel_id=1, source_target_pairs={{0,16},{2,18},{4,20},{6,22},{8,24},{10,26},{12,28},{14,30},{16,0},... | collective-permute-start | bytes 393224 | tf_op jit(solution)/shard_map/ppermute | solution.py:341
  920.0 28.8 %collective-permute-start.25 = (bf16[1,128,512]{2,1,0:T(8,128)(2,1)S(1)}, bf16[1,128,512]{2,1,0:T(8,128)(2,1)S(1)}, u32[]{:S(2)}, u32[]{:S(2)}) collective-permute-start(bf16[1,128,512]{2,1,0:T(8,128)(2,1)S(1)} %slice.538), channel_id=1, source_target_pairs={{0,16},{2,18},{4,20},{6,22},{8,24},{10,26},{12,28},{14,30},{16,0},... | collective-permute-start | bytes 393224 | tf_op jit(solution)/shard_map/ppermute | solution.py:341
  948.9 33.6 %collective-permute-start.43 = (bf16[2,64,2048]{2,1,0:T(8,128)(2,1)S(1)}, bf16[2,64,2048]{2,1,0:T(8,128)(2,1)S(1)}, u32[]{:S(2)}, u32[]{:S(2)}) collective-permute-start(bf16[2,64,2048]{2,1,0:T(8,128)(2,1)S(1)} %pad_maximum_fusion.52), channel_id=1, source_target_pairs={{0,8},{2,10},{4,12},{6,14},{8,0},{10,2},{12,4},{14,6},{16,24},{18,... | collective-permute-start | bytes 1572872 | tf_op jit(solution)/shard_map/ppermute | solution.py:341
  955.0 30.4 %collective-permute-start.51 = (bf16[2,128,1024]{2,1,0:T(8,128)(2,1)S(1)}, bf16[2,128,1024]{2,1,0:T(8,128)(2,1)S(1)}, u32[]{:S(2)}, u32[]{:S(2)}) collective-permute-start(bf16[2,128,1024]{2,1,0:T(8,128)(2,1)S(1)} %pad_maximum_fusion.53), channel_id=1, source_target_pairs={{0,8},{2,10},{4,12},{6,14},{8,0},{10,2},{12,4},{14,6},{16,24},{18,... | collective-permute-start | bytes 1572872 | tf_op jit(solution)/shard_map/ppermute | solution.py:341
  955.2 27.3 %collective-permute-start.35 = (bf16[2,128,512]{2,1,0:T(8,128)(2,1)S(1)}, bf16[2,128,512]{2,1,0:T(8,128)(2,1)S(1)}, u32[]{:S(2)}, u32[]{:S(2)}) collective-permute-start(bf16[2,128,512]{2,1,0:T(8,128)(2,1)S(1)} %pad_maximum_fusion.61), channel_id=1, source_target_pairs={{0,8},{2,10},{4,12},{6,14},{8,0},{10,2},{12,4},{14,6},{16,24},{18,... | collective-permute-start | bytes 786440 | tf_op jit(solution)/shard_map/ppermute | solution.py:341
  957.3 85.4 %collective-permute-start.98 = (bf16[8,64,2048]{2,1,0:T(8,128)(2,1)S(1)}, bf16[8,64,2048]{2,1,0:T(8,128)(2,1)S(1)}, u32[]{:S(2)}, u32[]{:S(2)}) collective-permute-start(bf16[8,64,2048]{2,1,0:T(8,128)(2,1)S(1)} %copy-done.28), channel_id=1, source_target_pairs={{0,2},{2,0},{4,6},{6,4},{8,10},{10,8},{12,14},{14,12},{16,18},{18,... | collective-permute-start | bytes 6291464 | tf_op jit(solution)/shard_map/ppermute | solution.py:341
  957.6 87.1 %collective-permute-start.106 = (bf16[8,128,1024]{2,1,0:T(8,128)(2,1)S(1)}, bf16[8,128,1024]{2,1,0:T(8,128)(2,1)S(1)}, u32[]{:S(2)}, u32[]{:S(2)}) collective-permute-start(bf16[8,128,1024]{2,1,0:T(8,128)(2,1)S(1)} %copy-done.29), channel_id=1, source_target_pairs={{0,4},{2,6},{4,0},{6,2},{8,12},{10,14},{12,8},{14,10},{16,20},{18,... | collective-permute-start | bytes 6291464 | tf_op jit(solution)/shard_map/ppermute | solution.py:341
  982.5 34.5 %collective-permute-start.36 = (bf16[4,128,512]{2,1,0:T(8,128)(2,1)S(1)}, bf16[4,128,512]{2,1,0:T(8,128)(2,1)S(1)}, u32[]{:S(2)}, u32[]{:S(2)}) collective-permute-start(bf16[4,128,512]{2,1,0:T(8,128)(2,1)S(1)} %pad_maximum_fusion.51), channel_id=1, source_target_pairs={{0,2},{2,0},{4,6},{6,4},{8,10},{10,8},{12,14},{14,12},{16,18},{18,... | collective-permute-start | bytes 1572872 | tf_op jit(solution)/shard_map/ppermute | solution.py:341
  990.6 37.9 %collective-permute-start.44 = (bf16[4,64,2048]{2,1,0:T(8,128)(2,1)S(1)}, bf16[4,64,2048]{2,1,0:T(8,128)(2,1)S(1)}, u32[]{:S(2)}, u32[]{:S(2)}) collective-permute-start(bf16[4,64,2048]{2,1,0:T(8,128)(2,1)S(1)} %pad_maximum_fusion.42), channel_id=1, source_target_pairs={{0,4},{2,6},{4,0},{6,2},{8,12},{10,14},{12,8},{14,10},{16,20},{18,... | collective-permute-start | bytes 3145736 | tf_op jit(solution)/shard_map/ppermute | solution.py:341
  990.9 48.7 %collective-permute-start.52 = (bf16[4,128,1024]{2,1,0:T(8,128)(2,1)S(1)}, bf16[4,128,1024]{2,1,0:T(8,128)(2,1)S(1)}, u32[]{:S(2)}, u32[]{:S(2)}) collective-permute-start(bf16[4,128,1024]{2,1,0:T(8,128)(2,1)S(1)} %pad_maximum_fusion.43), channel_id=1, source_target_pairs={{0,2},{2,0},{4,6},{6,4},{8,10},{10,8},{12,14},{14,12},{16,18},{18,... | collective-permute-start | bytes 3145736 | tf_op jit(solution)/shard_map/ppermute | solution.py:341
  1017.1 34.0 %collective-permute-start.74 = (bf16[8,128,512]{2,1,0:T(8,128)(2,1)S(1)}, bf16[8,128,512]{2,1,0:T(8,128)(2,1)S(1)}, u32[]{:S(2)}, u32[]{:S(2)}) collective-permute-start(bf16[8,128,512]{2,1,0:T(8,128)(2,1)S(1)} %pad_maximum_fusion.45.near_ref), channel_id=1, source_target_pairs={{0,4},{2,6},{4,0},{6,2},{8,12},{10,14},{12,8},{14,10},{16,20},{18,... | collective-permute-start | bytes 3145736 | tf_op jit(solution)/shard_map/ppermute | solution.py:341
  1028.6 66.2 %collective-permute-start.66 = (bf16[8,128,512]{2,1,0:T(8,128)(2,1)}, bf16[8,128,512]{2,1,0:T(8,128)(2,1)}, u32[]{:S(2)}, u32[]{:S(2)}) collective-permute-start(bf16[8,128,512]{2,1,0:T(8,128)(2,1)} %pad_maximum_fusion.44.near_ref), channel_id=1, source_target_pairs={{0,2},{2,0},{4,6},{6,4},{8,10},{10,8},{12,14},{14,12},{16,18},{18,... | collective-permute-start | bytes 3145736 | tf_op jit(solution)/shard_map/ppermute | solution.py:341
  1039.5 45.8 %collective-permute-start.28 = (bf16[4,128,512]{2,1,0:T(8,128)(2,1)}, bf16[4,128,512]{2,1,0:T(8,128)(2,1)}, u32[]{:S(2)}, u32[]{:S(2)}) collective-permute-start(bf16[4,128,512]{2,1,0:T(8,128)(2,1)} %pad_maximum_fusion.50), channel_id=1, source_target_pairs={{0,4},{2,6},{4,0},{6,2},{8,12},{10,14},{12,8},{14,10},{16,20},{18,... | collective-permute-start | bytes 1572872 | tf_op jit(solution)/shard_map/ppermute | solution.py:341
  1042.6 67.8 %collective-permute-start.37 = (bf16[8,128,512]{2,1,0:T(8,128)(2,1)S(1)}, bf16[8,128,512]{2,1,0:T(8,128)(2,1)}, u32[]{:S(2)}, u32[]{:S(2)}) collective-permute-start(bf16[8,128,512]{2,1,0:T(8,128)(2,1)S(1)} %pad_maximum_fusion.41.near_ref), channel_id=1, source_target_pairs={{0,4},{2,6},{4,0},{6,2},{8,12},{10,14},{12,8},{14,10},{16,20},{18,... | collective-permute-start | bytes 3145736 | tf_op jit(solution)/shard_map/ppermute | solution.py:341
  1044.7 108.4 %collective-permute-start.45 = (bf16[8,64,2048]{2,1,0:T(8,128)(2,1)}, bf16[8,64,2048]{2,1,0:T(8,128)(2,1)}, u32[]{:S(2)}, u32[]{:S(2)}) collective-permute-start(bf16[8,64,2048]{2,1,0:T(8,128)(2,1)} %pad_maximum_fusion.16.near_ref), channel_id=1, source_target_pairs={{0,2},{2,0},{4,6},{6,4},{8,10},{10,8},{12,14},{14,12},{16,18},{18,... | collective-permute-start | bytes 6291464 | tf_op jit(solution)/shard_map/ppermute | solution.py:341
  1051.0 91.1 %collective-permute-start.53 = (bf16[8,128,1024]{2,1,0:T(8,128)(2,1)}, bf16[8,128,1024]{2,1,0:T(8,128)(2,1)}, u32[]{:S(2)}, u32[]{:S(2)}) collective-permute-start(bf16[8,128,1024]{2,1,0:T(8,128)(2,1)} %pad_maximum_fusion.17.near_ref), channel_id=1, source_target_pairs={{0,4},{2,6},{4,0},{6,2},{8,12},{10,14},{12,8},{14,10},{16,20},{18,... | collective-permute-start | bytes 6291464 | tf_op jit(solution)/shard_map/ppermute | solution.py:341
  1087.5 38.9 %collective-permute-start.29 = (bf16[8,128,512]{2,1,0:T(8,128)(2,1)}, bf16[8,128,512]{2,1,0:T(8,128)(2,1)}, u32[]{:S(2)}, u32[]{:S(2)}) collective-permute-start(bf16[8,128,512]{2,1,0:T(8,128)(2,1)} %pad_maximum_fusion.40.near_ref), channel_id=1, source_target_pairs={{0,2},{2,0},{4,6},{6,4},{8,10},{10,8},{12,14},{14,12},{16,18},{18,... | collective-permute-start | bytes 3145736 | tf_op jit(solution)/shard_map/ppermute | solution.py:341
  (212 other events, 2956.3 us)

commit v2 on v1

--- a/solution.py
+++ b/solution.py
@@ -265,21 +265,26 @@
     return (collect(project(context, w_out)), (queries, keys, values, context, log_sums))
 
 
-def attention_backward(grad_out, query_in, memory_in, w_qkv, w_out, kept, meta, causal):
+def attention_backward(
+    grad_out, query_in, memory_in, w_qkv, w_out, kept, meta, causal, ticks, name
+):
     queries, keys, values, context, log_sums = kept
-    grad_full = spread(grad_out.astype(BF))
+    grad_full = ticks.mark(name + "_rows", spread(grad_out.astype(BF)))
     grad_context = back_project(grad_full, w_out).astype(BF)
     grad_w_out = weight_grad(grad_full, context).astype(BF)
     grad_q, grad_k, grad_v = attend_backward(
         meta, queries, keys, values, grad_context, context, log_sums, causal
     )
-    first = jnp.concatenate(
-        [weight_grad(query_in, grad_q).astype(BF), weight_grad(memory_in, grad_k).astype(BF)]
-    )
-    second = jnp.concatenate([weight_grad(memory_in, grad_v).astype(BF), grad_w_out])
+    grad_q = ticks.mark(name + "_kernel", grad_q)
+    weight_grads = (
+        weight_grad(query_in, grad_q).astype(BF),
+        weight_grad(memory_in, grad_k).astype(BF),
+        weight_grad(memory_in, grad_v).astype(BF),
+        grad_w_out,
+    )
     from_query = back_project(grad_q, w_qkv[0])
     from_memory = back_project(grad_k, w_qkv[1]) + back_project(grad_v, w_qkv[2])
-    return ((first, second), from_query, from_memory)
+    return (weight_grads, from_query, from_memory)
 
 
 def ffn_forward(normed_rows, w_in, w_out):
@@ -290,99 +295,71 @@
     return (result, (rows_full, zed, unit, w_in, w_out))
 
 
-def ffn_backward(grad_out, kept):
+def ffn_backward(grad_out, kept, ticks, name):
     rows, zed, unit, w_in, w_out = kept
-    grad_full = spread(grad_out.astype(BF))
+    grad_full = ticks.mark(name + "_rows", spread(grad_out.astype(BF)))
     grad_w_out = weight_grad(unit, grad_full).astype(BF)
     grad_unit = back_project(grad_full, w_out).astype(BF)
     grad_zed = (grad_unit.astype(F32) * gelu_slope(zed)).astype(BF)
+    grad_zed = ticks.mark(name + "_zed", grad_zed)
     grad_w_in = weight_grad(rows, grad_zed).astype(BF)
     grad_input = collect(back_project(grad_zed, w_in))
     return (grad_input, (grad_w_in, grad_w_out))
 
 
-def copy_out_kernel(index_ref, src_ref, keep_ref, send_ref):
-    step = pl.program_id(0)
-    half = pl.num_programs(0) // 2
-
-    @pl.when(step < half)
-    def _():
-        keep_ref[...] = src_ref[...]
-
-    @pl.when(step >= half)
-    def _():
-        send_ref[...] = src_ref[...]
-
-
-def copy_in_kernel(index_ref, near_ref, far_ref, out_ref):
-    step = pl.program_id(0)
-    half = pl.num_programs(0) // 2
-
-    @pl.when(step < half)
-    def _():
-        out_ref[...] = near_ref[...].astype(F32)
-
-    @pl.when(step >= half)
-    def _():
-        out_ref[...] = far_ref[...].astype(F32)
-
-
-def chunk_specs(count, rows, cols):
-    half = count // 2
-    block = (1, rows, cols)
-    whole = pl.BlockSpec(block, lambda step, index: (step ^ index[0], 0, 0))
-    near = pl.BlockSpec(block, lambda step, index: (jnp.minimum(step, half - 1), 0, 0))
-    far = pl.BlockSpec(block, lambda step, index: (jnp.maximum(step - half, 0), 0, 0))
-    return (whole, near, far)
-
-
 def partner(value, bit):
     count = lax.axis_size("dp")
     return lax.ppermute(value, "dp", [(at, at ^ (1 << bit)) for at in range(count)])
 
 
-def sum_over_pairs(value, first_bits):
-    count = lax.axis_size("dp")
-    levels = count.bit_length() - 1
+class Ticks:
+    def __init__(self):
+        self.last = lax.axis_index("dp") * 0
+        self.marks = {}
+
+    def mark(self, name, value):
+        self.last, value = lax.optimization_barrier((self.last, value))
+        self.marks[name] = self.last
+        return value
+
+
+def sum_over_pairs(low, high, first_bits, waits):
+    levels = lax.axis_size("dp").bit_length() - 1
     order = list(first_bits) + [bit for bit in range(levels) if bit not in first_bits]
+    waits = list(waits) + [0] * (2 * levels - len(waits))
     place = lax.axis_index("dp")
-    index = jnp.zeros((), jnp.int32)
-    for bit in order:
-        index = index * 2 + ((place >> bit) & 1)
-    index = index[None]
-    rows = value.shape[0] // count
-    cols = value.shape[1]
-    half = count // 2
-    whole, near, far = chunk_specs(count, rows, cols)
-    keep, send = pl.pallas_call(
-        copy_out_kernel,
-        grid_spec=pltpu.PrefetchScalarGridSpec(
-            num_scalar_prefetch=1, grid=(count,), in_specs=[whole], out_specs=[near, far]
-        ),
-        out_shape=[jax.ShapeDtypeStruct((half, rows, cols), BF)] * 2,
-        name="copy_out",
-    )(index, value.reshape(count, rows, cols))
-    for level, bit in enumerate(order):
+    upper = {bit: (place >> bit) & 1 for bit in order}
+    send = jnp.where(upper[order[0]] == 1, low, high)
+    at = upper[order[0]] + waits[0] == 1
+    summed = jnp.where(at, high, low) + partner(send, order[0])
+    for bit, wait in zip(order[1:], waits[1:levels]):
+        halves = summed.reshape(2, summed.shape[0] // 2, summed.shape[1])
+        send = lax.dynamic_index_in_dim(halves, 1 - upper[bit], 0, keepdims=False)
+        keep = lax.dynamic_index_in_dim(halves, upper[bit] + wait, 0, keepdims=False)
         summed = keep + partner(send, bit)
-        if level + 1 < levels:
-            middle = summed.shape[0] // 2
-            keep, send = summed[:middle], summed[middle:]
-    for bit in order[:0:-1]:
-        summed = jnp.concatenate([summed, partner(summed, bit)])
-    other = partner(summed, order[0])
-    result = pl.pallas_call(
-        copy_in_kernel,
-        grid_spec=pltpu.PrefetchScalarGridSpec(
-            num_scalar_prefetch=1, grid=(count,), in_specs=[near, far], out_specs=whole
-        ),
-        out_shape=jax.ShapeDtypeStruct((count, rows, cols), F32),
-        name="copy_in",
-    )(index, summed, other)
-    return result.reshape(value.shape)
-
-
-def sum_two(pair):
-    return (sum_over_pairs(pair[0], (0, 1)), sum_over_pairs(pair[1], (1, 0)))
+    for bit, wait in zip(order[::-1], waits[levels:]):
+        other = partner(summed, bit)
+        at = upper[bit] + wait == 1
+        halves = (jnp.where(at, other, summed), jnp.where(at, summed, other))
+        if bit != order[0]:
+            summed = jnp.concatenate(halves)
+    return (halves[0].astype(F32), halves[1].astype(F32))
+
+
+def sum_rows(value, first_bits, waits):
+    half = value.shape[0] // 2
+    return jnp.concatenate(sum_over_pairs(value[:half], value[half:], first_bits, waits))
+
+
+def sum_ffn(pair, waits=()):
+    return (sum_rows(pair[0], (0, 1), waits), sum_rows(pair[1], (1, 0), waits))
+
+
+def sum_attention(grads, waits=()):
+    query, key, value, out = grads
+    query, key = sum_over_pairs(query, key, (0, 1), waits)
+    value, out = sum_over_pairs(value, out, (1, 0), waits)
+    return (jnp.stack([query, key, value]), out.T)
 
 
 def sum_everywhere(value):
@@ -393,15 +370,6 @@
                 value, axis, [(at, at ^ (1 << bit)) for at in range(count)]
             )
     return value
-
-
-def split_attention(pair):
-    first, second = pair
-    rows = first.shape[0] // 2
-    return (
-        jnp.concatenate([first, second[:rows]]).reshape(3, rows, first.shape[1]),
-        second[rows:].T,
-    )
 
 
 def on_device(
@@ -462,11 +430,11 @@
     ffn_dec, keep_dec_ffn = ffn_forward(ln_b3.astype(BF), dec_ffn_in, dec_ffn_out)
     resid_three = resid_two + ffn_dec
     ln_final, nm_final, inv_final = norm_forward(resid_three, dec_gain[3], dec_bias[3])
+    ticks = Ticks()
     grad_r3, gain_final, bias_final = norm_backward(
         dec_cot[0].astype(F32), nm_final, inv_final, dec_gain[3]
     )
-    grad_b3, dec_ffn_grads = ffn_backward(grad_r3, keep_dec_ffn)
-    dec_ffn_sums = sum_two(dec_ffn_grads)
+    grad_b3, dec_ffn_grads = ffn_backward(grad_r3, keep_dec_ffn, ticks, "dec_ffn")
     part_r2, gain_b3, bias_b3 = norm_backward(grad_b3, nm_b3, inv_b3, dec_gain[2])
     grad_r2 = grad_r3 + part_r2
     cross_grads, from_query, from_memory = attention_backward(
@@ -478,30 +446,61 @@
         keep_cross,
         src_meta,
         False,
-    )
-    cross_sums = split_attention(sum_two(cross_grads))
+        ticks,
+        "cross",
+    )
     grad_memory = enc_cot[0].astype(F32) + collect(from_memory)
     grad_h2, gain_mem, bias_mem = norm_backward(grad_memory, nm_mem, inv_mem, enc_gain[2])
-    grad_a2, enc_ffn_grads = ffn_backward(grad_h2, keep_enc_ffn)
-    enc_ffn_sums = sum_two(enc_ffn_grads)
+    grad_a2, enc_ffn_grads = ffn_backward(grad_h2, keep_enc_ffn, ticks, "enc_ffn")
     part_r1, gain_b2, bias_b2 = norm_backward(collect(from_query), nm_b2, inv_b2, dec_gain[1])
     grad_r1 = grad_r2 + part_r1
     self_grads, self_query, self_memory = attention_backward(
-        grad_r1, dec_rows, dec_rows, dec_qkv, dec_self_out, keep_self, tgt_meta, True
-    )
-    self_sums = split_attention(sum_two(self_grads))
+        grad_r1,
+        dec_rows,
+        dec_rows,
+        dec_qkv,
+        dec_self_out,
+        keep_self,
+        tgt_meta,
+        True,
+        ticks,
+        "self",
+    )
     grad_b1 = collect(self_query + self_memory)
     part_tgt, gain_b1, bias_b1 = norm_backward(grad_b1, nm_b1, inv_b1, dec_gain[0])
     grad_tgt = grad_r1 + part_tgt
     part_h1, gain_a2, bias_a2 = norm_backward(grad_a2, nm_a2, inv_a2, enc_gain[1])
     grad_h1 = grad_h2 + part_h1
     enc_grads, enc_query, enc_memory = attention_backward(
-        grad_h1, enc_rows, enc_rows, enc_qkv, enc_out_w, keep_enc_attn, src_meta, False
-    )
-    enc_sums = split_attention(sum_two(enc_grads))
+        grad_h1,
+        enc_rows,
+        enc_rows,
+        enc_qkv,
+        enc_out_w,
+        keep_enc_attn,
+        src_meta,
+        False,
+        ticks,
+        "enc",
+    )
     grad_a1 = collect(enc_query + enc_memory)
     part_src, gain_a1, bias_a1 = norm_backward(grad_a1, nm_a1, inv_a1, enc_gain[0])
     grad_src = grad_h1 + part_src
+    marks = ticks.marks
+    early = (
+        marks["cross_kernel"],
+        marks["enc_ffn_rows"],
+        marks["enc_ffn_zed"],
+        marks["self_rows"],
+        marks["self_kernel"],
+        marks["enc_rows"],
+        marks["enc_kernel"],
+    )
+    dec_ffn_sums = sum_ffn(dec_ffn_grads, early)
+    cross_sums = sum_attention(cross_grads, early[3:])
+    enc_ffn_sums = sum_ffn(enc_ffn_grads, early[5:])
+    self_sums = sum_attention(self_grads, early[6:])
+    enc_sums = sum_attention(enc_grads)
     small = sum_everywhere(
         jnp.stack(
             [

time: 1190 us -> 1060 us (0.89)
  Pallas kernels: 351 us -> 149 us
  waiting for transfers between devices: 310 us -> 379 us
  other arithmetic: 135 us -> 190 us
  starting transfers between devices: 108 us -> 74.3 us
  matrix products: 194 us -> 175 us
    pallas_call x20 -> x0, Pallas kernels: 203 us -> none  [the longest x10 104 us: sum_over_pairs(): pl.pallas_call(copy_in_kernel, grid_spec=pltpu.PrefetchScalarGridSpec(num...]
    ppermute x80, waiting for transfers between devices: 286 us -> 333 us  [partner(): lax.ppermute(value, 'dp', [(at, at ^ 1 << bit) for at in range(count)])]
    select_n x0 -> x38, other arithmetic: none -> 34.1 us  [the longest x34 27.8 us: sum_over_pairs(): halves = (jnp.where(at, other, summed), jnp.where(at, summed, other))]
    ppermute x80, starting transfers between devices: 98 us -> 67.2 us  [partner(): lax.ppermute(value, 'dp', [(at, at ^ 1 << bit) for at in range(count)])]
    ppermute x5, waiting for transfers between devices: 12.4 us -> 40.3 us  [sum_everywhere(): lax.ppermute(value, axis, [(at, at ^ 1 << bit) for at in range(count)])]
    slice x36 -> x0, local copies, waits for them, and re-layouts: 24.4 us -> none  [the longest x6 18.4 us: split_attention(): second[rows:]]
    add x0 -> x10, other arithmetic: none -> 18.8 us  [sum_over_pairs(): summed = jnp.where(at, high, low) + partner(send, order[0])]
    dot_general x48, matrix products: 194 us -> 175 us  [dot(): lax.dot_general(left, right, (((left_dim,), (right_dim,)), ((), ())), pre...]
  transfers between devices with their start and end apart: 107 -> 107, of which waited for: 37 -> 48; matrix products, arithmetic and copies ran while one was open for 27% -> 34% of each run, Pallas kernels for 27% -> 12%
where the time goes in v2:
time: 1060 us; the launch traced here: 1040 us
  waiting for transfers between devices  379 us (36%)
  other arithmetic  190 us (18%)
  matrix products  175 us (17%)
  Pallas kernels  149 us (14%)
  starting transfers between devices  74.3 us (7%)
  local copies, waits for them, and re-layouts  67.4 us (6%)
    ppermute x80, waiting for transfers between devices, partner(): lax.ppermute(value, 'dp', [(at, at ^ 1 << bit) for at in range(count)])  333 us
    dot_general x48, matrix products, dot(): lax.dot_general(left, right, (((left_dim,), (right_dim,)), ((), ())), pre...  175 us
    pallas_call x3, Pallas kernels, attend_backward(): pl.pallas_call(partial(backward_kernel, causal=causal), grid_spec=pltpu.P...  86 us
    ppermute x80, starting transfers between devices, partner(): lax.ppermute(value, 'dp', [(at, at ^ 1 << bit) for at in range(count)])  67.2 us
    pallas_call x3, Pallas kernels, attend_forward(): pl.pallas_call(partial(forward_kernel, causal=causal), grid_spec=pltpu.Pr...  62.9 us
    ppermute x5, waiting for transfers between devices, sum_everywhere(): lax.ppermute(value, axis, [(at, at ^ 1 << bit) for at in range(count)])  40.3 us
    unnamed x465, local copies, waits for them, and re-layouts  39.9 us
    select_n x34, other arithmetic, sum_over_pairs(): halves = (jnp.where(at, other, summed), jnp.where(at, summed, other))  27.8 us
  transfers between devices with their start and end apart: 107, of which 48 were waited for; matrix products, arithmetic and copies ran while one was open for 34% of the time, Pallas kernels for 12%

profile of v2, /device:TPU:0, one launch (start us, length us, event | category | flops | bytes accessed | tf_op | source)
XLA Modules:
  0.0 1040.4 jit_solution(12217297767652787383)
XLA Ops:
  9.1 4.2 convolution_convert_fusion.26.k_ref
  13.3 3.8 convolution_convert_fusion.25.v_ref
  20.9 21.0 %attend_forward.3 = (bf16[1024,512]{1,0:T(8,128)(2,1)}, f32[4,2,1024]{2,1,0:T(2,128)}) custom-call(s32[2]{0:T(128)} %pad_add_fusion.meta_ref, bf16[1024,512]{1,0:T(8,128)(2,1)} %convolution_convert_fusion.27.q_ref, bf16[1024,512]{1,0:T(8,128)(2,1)} %convolution_convert_fusion.26.k_ref, bf16[1024,512]{1,0:T(8,128)(2,1)} %convolution_convert_fusion.25.v_ref), custom_call_target="tpu_custom_call" | custom-call | tf_op jit(solution)/shard_map/attend_forward/pallas_call | solution.py:213
  59.9 20.9 %attend_forward.4 = (bf16[1024,512]{1,0:T(8,128)(2,1)}, f32[4,2,1024]{2,1,0:T(2,128)}) custom-call(s32[2]{0:T(128)} %pad_add_fusion.1.meta_ref, bf16[1024,512]{1,0:T(8,128)(2,1)} %convolution_convert_fusion.24.q_ref, bf16[1024,512]{1,0:T(8,128)(2,1)} %convolution_convert_fusion.23.k_ref, bf16[1024,512]{1,0:T(8,128)(2,1)} %convolution_convert_fusion.22.v_ref), custom_call_target="tpu_custom_call" | custom-call | tf_op jit(solution)/shard_map/attend_forward/pallas_call | solution.py:213
  84.2 8.7 multiply_convert_fusion.1
  92.9 4.5 fusion.138
  111.3 21.0 %attend_forward.5 = (bf16[1024,512]{1,0:T(8,128)(2,1)}, f32[4,2,1024]{2,1,0:T(2,128)}) custom-call(s32[2]{0:T(128)} %pad_add_fusion.meta_ref, bf16[1024,512]{1,0:T(8,128)(2,1)} %convolution_convert_fusion.21.q_ref, bf16[1024,512]{1,0:T(8,128)(2,1)} %convolution_convert_fusion.20.k_ref, bf16[1024,512]{1,0:T(8,128)(2,1)} %convolution_convert_fusion.19.v_ref), custom_call_target="tpu_custom_call" | custom-call | tf_op jit(solution)/shard_map/attend_forward/pallas_call | solution.py:213
  142.5 7.2 multiply_convert_fusion
  149.7 4.6 fusion.141
  176.7 9.2 fusion.5
  185.9 4.5 fusion.142
  191.0 5.4 convolution_convert_fusion
  206.9 4.7 convolution_convert_fusion.1
  222.1 28.1 %attend_backward.3 = (bf16[1024,512]{1,0:T(8,128)(2,1)}, bf16[1024,512]{1,0:T(8,128)(2,1)}, bf16[1024,512]{1,0:T(8,128)(2,1)}) custom-call(s32[2]{0:T(128)} %pad_add_fusion.meta_ref, bf16[1024,512]{1,0:T(8,128)(2,1)} %convolution_convert_fusion.21.q_ref, bf16[1024,512]{1,0:T(8,128)(2,1)} %convolution_convert_fusion.20.k_ref, ...), custom_call_target="tpu_custom_call" | custom-call | tf_op jit(solution)/shard_map/attend_backward/pallas_call | solution.py:234
  291.1 8.4 fusion.11
  303.7 29.8 %attend_backward.4 = (bf16[1024,512]{1,0:T(8,128)(2,1)}, bf16[1024,512]{1,0:T(8,128)(2,1)}, bf16[1024,512]{1,0:T(8,128)(2,1)}) custom-call(s32[2]{0:T(128)} %pad_add_fusion.1.meta_ref, bf16[1024,512]{1,0:T(8,128)(2,1)} %convolution_convert_fusion.24.q_ref, bf16[1024,512]{1,0:T(8,128)(2,1)} %convolution_convert_fusion.23.k_ref, ...), custom_call_target="tpu_custom_call" | custom-call | tf_op jit(solution)/shard_map/attend_backward/pallas_call | solution.py:234
  343.0 6.2 convolution_convert_fusion.2
  356.8 8.2 fusion.143
  380.0 7.0 convolution_convert_fusion.3
  387.1 4.7 broadcast_select_fusion.24
  391.8 3.8 broadcast_select_fusion.21
  409.5 8.0 collective-permute-done.94
  417.6 13.7 %collective-permute-done.102 = bf16[128,1024]{1,0:T(8,128)(2,1)S(1)} collective-permute-done((bf16[128,1024]{1,0:T(8,128)(2,1)S(1)}, bf16[128,1024]{1,0:T(8,128)(2,1)S(1)}, u32[]{:S(2)}, u32[]{:S(2)}) %collective-permute-start.102) | collective-permute-done | bytes 262176 | tf_op jit(solution)/shard_map/ppermute | solution.py:312
  439.8 3.9 fusion.116
  443.7 13.7 %collective-permute-done.95 = bf16[64,2048]{1,0:T(8,128)(2,1)S(1)} collective-permute-done((bf16[64,2048]{1,0:T(8,128)(2,1)S(1)}, bf16[64,2048]{1,0:T(8,128)(2,1)S(1)}, u32[]{:S(2)}, u32[]{:S(2)}) %collective-permute-start.95) | collective-permute-done | bytes 262176 | tf_op jit(solution)/shard_map/ppermute | solution.py:312
  466.9 8.4 collective-permute-done.96
  483.1 5.9 collective-permute-done.77
  493.8 28.1 %attend_backward.5 = (bf16[1024,512]{1,0:T(8,128)(2,1)}, bf16[1024,512]{1,0:T(8,128)(2,1)}, bf16[1024,512]{1,0:T(8,128)(2,1)}) custom-call(s32[2]{0:T(128)} %pad_add_fusion.meta_ref, bf16[1024,512]{1,0:T(8,128)(2,1)} %convolution_convert_fusion.27.q_ref, bf16[1024,512]{1,0:T(8,128)(2,1)} %convolution_convert_fusion.26.k_ref, ...), custom_call_target="tpu_custom_call" | custom-call | tf_op jit(solution)/shard_map/attend_backward/pallas_call | solution.py:234
  540.4 4.3 broadcast_select_fusion.25
  547.6 4.1 broadcast_select_fusion.22
  568.9 5.4 collective-permute-done.79
  574.4 7.0 collective-permute-done.87
  591.3 8.2 collective-permute-done.69
  599.9 7.5 collective-permute-done.61
  608.8 6.3 collective-permute-done.70
  615.1 8.3 collective-permute-done.62
  628.3 31.3 %collective-permute-done.81 = bf16[512,512]{1,0:T(8,128)(2,1)S(1)} collective-permute-done((bf16[512,512]{1,0:T(8,128)(2,1)S(1)}, bf16[512,512]{1,0:T(8,128)(2,1)S(1)}, u32[]{:S(2)}, u32[]{:S(2)}) %collective-permute-start.81) | collective-permute-done | bytes 524320 | tf_op jit(solution)/shard_map/ppermute | solution.py:312
  661.2 5.2 collective-permute-done.71
  670.6 5.4 collective-permute-done.63
  694.4 20.8 %collective-permute-done.47 = bf16[512,1024]{1,0:T(8,128)(2,1)} collective-permute-done((bf16[512,1024]{1,0:T(8,128)(2,1)}, bf16[512,1024]{1,0:T(8,128)(2,1)}, u32[]{:S(2)}, u32[]{:S(2)}) %collective-permute-start.47) | collective-permute-done | bytes 1048608 | tf_op jit(solution)/shard_map/ppermute | solution.py:312
  721.5 27.4 %collective-permute-done.55 = f32[14,1024]{1,0:T(8,128)S(1)} collective-permute-done((f32[14,1024]{1,0:T(8,128)S(1)}, f32[14,1024]{1,0:T(8,128)S(1)}, u32[]{:S(2)}, u32[]{:S(2)}) %collective-permute-start.55) | collective-permute-done | bytes 57376 | tf_op jit(solution)/shard_map/ppermute | solution.py:369
  753.4 4.7 collective-permute-done.57
  758.5 6.9 collective-permute-done.64
  766.5 4.6 collective-permute-done.58
  775.9 10.0 collective-permute-done.48
  786.2 10.1 collective-permute-done.40
  800.3 4.8 collective-permute-done.24
  808.6 11.8 %collective-permute-done.49 = bf16[128,1024]{1,0:T(8,128)(2,1)S(1)} collective-permute-done((bf16[128,1024]{1,0:T(8,128)(2,1)S(1)}, bf16[128,1024]{1,0:T(8,128)(2,1)S(1)}, u32[]{:S(2)}, u32[]{:S(2)}) %collective-permute-start.49) | collective-permute-done | bytes 262176 | tf_op jit(solution)/shard_map/ppermute | solution.py:312
  821.3 10.7 %collective-permute-done.41 = bf16[64,2048]{1,0:T(8,128)(2,1)S(1)} collective-permute-done((bf16[64,2048]{1,0:T(8,128)(2,1)S(1)}, bf16[64,2048]{1,0:T(8,128)(2,1)S(1)}, u32[]{:S(2)}, u32[]{:S(2)}) %collective-permute-start.41) | collective-permute-done | bytes 262176 | tf_op jit(solution)/shard_map/ppermute | solution.py:312
  833.8 4.8 collective-permute-done.33
  838.7 11.0 %collective-permute-done.25 = bf16[128,512]{1,0:T(8,128)(2,1)S(1)} collective-permute-done((bf16[128,512]{1,0:T(8,128)(2,1)S(1)}, bf16[128,512]{1,0:T(8,128)(2,1)S(1)}, u32[]{:S(2)}, u32[]{:S(2)}) %collective-permute-start.25) | collective-permute-done | bytes 131104 | tf_op jit(solution)/shard_map/ppermute | solution.py:312
  856.0 7.9 collective-permute-done.34
  864.0 8.5 collective-permute-done.26
  893.6 5.2 collective-permute-done.27
  899.2 8.3 collective-permute-done.43
  908.5 4.6 collective-permute-done.51
  915.3 6.9 collective-permute-done.36
  925.0 12.0 %collective-permute-done.28 = bf16[512,512]{1,0:T(8,128)(2,1)S(1)} collective-permute-done((bf16[512,512]{1,0:T(8,128)(2,1)S(1)}, bf16[512,512]{1,0:T(8,128)(2,1)S(1)}, u32[]{:S(2)}, u32[]{:S(2)}) %collective-permute-start.28) | collective-permute-done | bytes 524320 | tf_op jit(solution)/shard_map/ppermute | solution.py:312
  965.9 4.5 maximum_convert_fusion.3
  973.9 4.3 maximum_convert_fusion.2
  978.2 6.3 collective-permute-done.37
  996.0 29.7 %collective-permute-done.45 = bf16[512,2048]{1,0:T(8,128)(2,1)} collective-permute-done((bf16[512,2048]{1,0:T(8,128)(2,1)}, bf16[512,2048]{1,0:T(8,128)(2,1)}, u32[]{:S(2)}, u32[]{:S(2)}) %collective-permute-start.45) | collective-permute-done | bytes 2097184 | tf_op jit(solution)/shard_map/ppermute | solution.py:312
  1028.5 4.3 maximum_convert_fusion
  1035.7 4.5 maximum_convert_fusion.1
  (914 shorter events, 409.6 us)
Async XLA Ops:
  7.6 38.9 %collective-permute-start.4 = (bf16[512,1024]{0,1:T(8,128)(2,1)S(1)}, bf16[512,1024]{0,1:T(8,128)(2,1)}, u32[]{:S(2)}, u32[]{:S(2)}) collective-permute-start(bf16[512,1024]{0,1:T(8,128)(2,1)S(1)} %fusion.34), channel_id=1, source_target_pairs={{0,1},{1,0},{2,3},{3,2},{4,5},{5,4},{6,7},{7,6},{8,9},{9,8},{10,11... | collective-permute-start | bytes 3145736 | tf_op jit(solution)/shard_map/ppermute | solution.py:70
  52.4 31.8 %collective-permute-start.2 = (bf16[512,1024]{1,0:T(8,128)(2,1)}, bf16[512,1024]{1,0:T(8,128)(2,1)}, u32[]{:S(2)}, u32[]{:S(2)}) collective-permute-start(bf16[512,1024]{1,0:T(8,128)(2,1)} %add_convert_fusion.4), channel_id=1, source_target_pairs={{0,1},{1,0},{2,3},{3,2},{4,5},{5,4},{6,7},{7,6},{8,9},{9,8},{10,11... | collective-permute-start | bytes 3145736 | tf_op jit(solution)/shard_map/ppermute | solution.py:70
  84.0 14.2 %collective-permute-start.5 = (bf16[512,1024]{0,1:T(8,128)(2,1)S(1)}, bf16[512,1024]{0,1:T(8,128)(2,1)S(1)}, u32[]{:S(2)}, u32[]{:S(2)}) collective-permute-start(bf16[512,1024]{0,1:T(8,128)(2,1)S(1)} %slice.469), channel_id=1, source_target_pairs={{0,1},{1,0},{2,3},{3,2},{4,5},{5,4},{6,7},{7,6},{8,9},{9,8},{10,11... | collective-permute-start | bytes 3145736 | tf_op jit(solution)/shard_map/ppermute | solution.py:70
  199.2 70.5 %collective-permute-start.99 = (bf16[1024,1024]{1,0:T(8,128)(2,1)}, bf16[1024,1024]{1,0:T(8,128)(2,1)}, u32[]{:S(2)}, u32[]{:S(2)}) collective-permute-start(bf16[1024,1024]{1,0:T(8,128)(2,1)} %broadcast_select_fusion.2), channel_id=1, source_target_pairs={{0,4},{2,6},{4,0},{6,2},{8,12},{10,14},{12,8},{14,10},{16,20},{18,... | collective-permute-start | bytes 6291464 | tf_op jit(solution)/shard_map/ppermute | solution.py:312
  214.3 59.6 %collective-permute-start.91 = (bf16[512,2048]{1,0:T(8,128)(2,1)}, bf16[512,2048]{1,0:T(8,128)(2,1)}, u32[]{:S(2)}, u32[]{:S(2)}) collective-permute-start(bf16[512,2048]{1,0:T(8,128)(2,1)} %broadcast_select_fusion.8), channel_id=1, source_target_pairs={{0,2},{2,0},{4,6},{6,4},{8,10},{10,8},{12,14},{14,12},{16,18},{18,... | collective-permute-start | bytes 6291464 | tf_op jit(solution)/shard_map/ppermute | solution.py:312
  257.2 76.3 %collective-permute-start.75 = (bf16[1024,512]{1,0:T(8,128)(2,1)}, bf16[1024,512]{1,0:T(8,128)(2,1)}, u32[]{:S(2)}, u32[]{:S(2)}) collective-permute-start(bf16[1024,512]{1,0:T(8,128)(2,1)} %get-tuple-element.265), channel_id=1, source_target_pairs={{0,2},{2,0},{4,6},{6,4},{8,10},{10,8},{12,14},{14,12},{16,18},{18,... | collective-permute-start | bytes 3145736 | tf_op jit(solution)/shard_map/ppermute | solution.py:312
  263.9 76.7 %collective-permute-start.83 = (bf16[1024,512]{1,0:T(8,128)(2,1)}, bf16[1024,512]{1,0:T(8,128)(2,1)}, u32[]{:S(2)}, u32[]{:S(2)}) collective-permute-start(bf16[1024,512]{1,0:T(8,128)(2,1)} %get-tuple-element.263), channel_id=1, source_target_pairs={{0,4},{2,6},{4,0},{6,2},{8,12},{10,14},{12,8},{14,10},{16,20},{18,... | collective-permute-start | bytes 3145736 | tf_op jit(solution)/shard_map/ppermute | solution.py:312
  265.9 17.8 %collective-permute-start.17 = (bf16[512,1024]{0,1:T(8,128)(2,1)S(1)}, bf16[512,1024]{0,1:T(8,128)(2,1)S(1)}, u32[]{:S(2)}, u32[]{:S(2)}) collective-permute-start(bf16[512,1024]{0,1:T(8,128)(2,1)S(1)} %slice.463), channel_id=1, source_target_pairs={{0,1},{1,0},{2,3},{3,2},{4,5},{5,4},{6,7},{7,6},{8,9},{9,8},{10,11... | collective-permute-start | bytes 3145736 | tf_op jit(solution)/shard_map/ppermute | solution.py:70
  273.9 75.4 %collective-permute-start.100 = (bf16[512,1024]{1,0:T(8,128)(2,1)}, bf16[512,1024]{1,0:T(8,128)(2,1)}, u32[]{:S(2)}, u32[]{:S(2)}) collective-permute-start(bf16[512,1024]{1,0:T(8,128)(2,1)} %dynamic-slice_bitcast_fusion), channel_id=1, source_target_pairs={{0,2},{2,0},{4,6},{6,4},{8,10},{10,8},{12,14},{14,12},{16,18},{18,... | collective-permute-start | bytes 3145736 | tf_op jit(solution)/shard_map/ppermute | solution.py:312
  278.3 57.7 %collective-permute-start.92 = (bf16[256,2048]{1,0:T(8,128)(2,1)}, bf16[256,2048]{1,0:T(8,128)(2,1)}, u32[]{:S(2)}, u32[]{:S(2)}) collective-permute-start(bf16[256,2048]{1,0:T(8,128)(2,1)} %dynamic-slice_bitcast_fusion.1), channel_id=1, source_target_pairs={{0,4},{2,6},{4,0},{6,2},{8,12},{10,14},{12,8},{14,10},{16,20},{18,... | collective-permute-start | bytes 3145736 | tf_op jit(solution)/shard_map/ppermute | solution.py:312
  352.5 46.4 %collective-permute-start.101 = (bf16[256,1024]{1,0:T(8,128)(2,1)}, bf16[256,1024]{1,0:T(8,128)(2,1)}, u32[]{:S(2)}, u32[]{:S(2)}) collective-permute-start(bf16[256,1024]{1,0:T(8,128)(2,1)} %dynamic-slice_bitcast_fusion.4), channel_id=1, source_target_pairs={{0,8},{2,10},{4,12},{6,14},{8,0},{10,2},{12,4},{14,6},{16,24},{18,... | collective-permute-start | bytes 1572872 | tf_op jit(solution)/shard_map/ppermute | solution.py:312
  354.1 43.0 %collective-permute-start.93 = (bf16[128,2048]{1,0:T(8,128)(2,1)}, bf16[128,2048]{1,0:T(8,128)(2,1)}, u32[]{:S(2)}, u32[]{:S(2)}) collective-permute-start(bf16[128,2048]{1,0:T(8,128)(2,1)} %dynamic-slice_bitcast_fusion.5), channel_id=1, source_target_pairs={{0,8},{2,10},{4,12},{6,14},{8,0},{10,2},{12,4},{14,6},{16,24},{18,... | collective-permute-start | bytes 1572872 | tf_op jit(solution)/shard_map/ppermute | solution.py:312
  354.5 49.6 %collective-permute-start.84 = (bf16[512,512]{1,0:T(8,128)(2,1)}, bf16[512,512]{1,0:T(8,128)(2,1)}, u32[]{:S(2)}, u32[]{:S(2)}) collective-permute-start(bf16[512,512]{1,0:T(8,128)(2,1)} %dynamic-slice_bitcast_fusion.6), channel_id=1, source_target_pairs={{0,2},{2,0},{4,6},{6,4},{8,10},{10,8},{12,14},{14,12},{16,18},{18,... | collective-permute-start | bytes 1572872 | tf_op jit(solution)/shard_map/ppermute | solution.py:312
  355.4 46.0 %collective-permute-start.76 = (bf16[512,512]{1,0:T(8,128)(2,1)}, bf16[512,512]{1,0:T(8,128)(2,1)}, u32[]{:S(2)}, u32[]{:S(2)}) collective-permute-start(bf16[512,512]{1,0:T(8,128)(2,1)} %dynamic-slice_bitcast_fusion.7), channel_id=1, source_target_pairs={{0,4},{2,6},{4,0},{6,2},{8,12},{10,14},{12,8},{14,10},{16,20},{18,... | collective-permute-start | bytes 1572872 | tf_op jit(solution)/shard_map/ppermute | solution.py:312
  366.2 65.8 %collective-permute-start.16 = (bf16[512,1024]{1,0:T(8,128)(2,1)}, bf16[512,1024]{1,0:T(8,128)(2,1)}, u32[]{:S(2)}, u32[]{:S(2)}) collective-permute-start(bf16[512,1024]{1,0:T(8,128)(2,1)} %slice.464), channel_id=1, source_target_pairs={{0,1},{1,0},{2,3},{3,2},{4,5},{5,4},{6,7},{7,6},{8,9},{9,8},{10,11... | collective-permute-start | bytes 3145736 | tf_op jit(solution)/shard_map/ppermute | solution.py:70
  397.1 130.0 %collective-permute-start.67 = (bf16[1024,512]{1,0:T(8,128)(2,1)}, bf16[1024,512]{1,0:T(8,128)(2,1)}, u32[]{:S(2)}, u32[]{:S(2)}) collective-permute-start(bf16[1024,512]{1,0:T(8,128)(2,1)} %get-tuple-element.259), channel_id=1, source_target_pairs={{0,4},{2,6},{4,0},{6,2},{8,12},{10,14},{12,8},{14,10},{16,20},{18,... | collective-permute-start | bytes 3145736 | tf_op jit(solution)/shard_map/ppermute | solution.py:312
  398.9 156.2 %collective-permute-start.59 = (bf16[1024,512]{1,0:T(8,128)(2,1)}, bf16[1024,512]{1,0:T(8,128)(2,1)}, u32[]{:S(2)}, u32[]{:S(2)}) collective-permute-start(bf16[1024,512]{1,0:T(8,128)(2,1)} %get-tuple-element.261), channel_id=1, source_target_pairs={{0,2},{2,0},{4,6},{6,4},{8,10},{10,8},{12,14},{14,12},{16,18},{18,... | collective-permute-start | bytes 3145736 | tf_op jit(solution)/shard_map/ppermute | solution.py:312
  401.4 74.4 %collective-permute-start.46 = (bf16[1024,1024]{1,0:T(8,128)(2,1)}, bf16[1024,1024]{1,0:T(8,128)(2,1)}, u32[]{:S(2)}, u32[]{:S(2)}) collective-permute-start(bf16[1024,1024]{1,0:T(8,128)(2,1)} %broadcast_select_fusion.5), channel_id=1, source_target_pairs={{0,4},{2,6},{4,0},{6,2},{8,12},{10,14},{12,8},{14,10},{16,20},{18,... | collective-permute-start | bytes 6291464 | tf_op jit(solution)/shard_map/ppermute | solution.py:312
  432.1 28.8 %collective-permute-start.103 = (bf16[128,1024]{1,0:T(8,128)(2,1)}, bf16[128,1024]{1,0:T(8,128)(2,1)}, u32[]{:S(2)}, u32[]{:S(2)}) collective-permute-start(bf16[128,1024]{1,0:T(8,128)(2,1)} %bitcast_add_fusion.14), channel_id=1, source_target_pairs={{0,16},{2,18},{4,20},{6,22},{8,24},{10,26},{12,28},{14,30},{16,0},... | collective-permute-start | bytes 786440 | tf_op jit(solution)/shard_map/ppermute | solution.py:312
  435.3 22.1 %collective-permute-start.95 = (bf16[64,2048]{1,0:T(8,128)(2,1)S(1)}, bf16[64,2048]{1,0:T(8,128)(2,1)S(1)}, u32[]{:S(2)}, u32[]{:S(2)}) collective-permute-start(bf16[64,2048]{1,0:T(8,128)(2,1)S(1)} %bitcast_add_fusion.15), channel_id=1, source_target_pairs={{0,16},{2,18},{4,20},{6,22},{8,24},{10,26},{12,28},{14,30},{16,0},... | collective-permute-start | bytes 786440 | tf_op jit(solution)/shard_map/ppermute | solution.py:312
  460.9 14.3 %collective-permute-start.96 = (bf16[128,2048]{1,0:T(8,128)(2,1)S(1)}, bf16[128,2048]{1,0:T(8,128)(2,1)S(1)}, u32[]{:S(2)}, u32[]{:S(2)}) collective-permute-start(bf16[128,2048]{1,0:T(8,128)(2,1)S(1)} %pad_maximum_fusion.39), channel_id=1, source_target_pairs={{0,8},{2,10},{4,12},{6,14},{8,0},{10,2},{12,4},{14,6},{16,24},{18,... | collective-permute-start | bytes 1572872 | tf_op jit(solution)/shard_map/ppermute | solution.py:312
  462.9 81.8 %collective-permute-start.38 = (bf16[512,2048]{1,0:T(8,128)(2,1)}, bf16[512,2048]{1,0:T(8,128)(2,1)}, u32[]{:S(2)}, u32[]{:S(2)}) collective-permute-start(bf16[512,2048]{1,0:T(8,128)(2,1)} %broadcast_select_fusion.11), channel_id=1, source_target_pairs={{0,2},{2,0},{4,6},{6,4},{8,10},{10,8},{12,14},{14,12},{16,18},{18,... | collective-permute-start | bytes 6291464 | tf_op jit(solution)/shard_map/ppermute | solution.py:312
  475.2 15.1 %collective-permute-start.85 = (bf16[256,512]{1,0:T(8,128)(2,1)}, bf16[256,512]{1,0:T(8,128)(2,1)S(1)}, u32[]{:S(2)}, u32[]{:S(2)}) collective-permute-start(bf16[256,512]{1,0:T(8,128)(2,1)} %dynamic-slice_bitcast_fusion.16), channel_id=1, source_target_pairs={{0,8},{2,10},{4,12},{6,14},{8,0},{10,2},{12,4},{14,6},{16,24},{18,... | collective-permute-start | bytes 786440 | tf_op jit(solution)/shard_map/ppermute | solution.py:312
  488.9 36.6 %collective-permute-start.104 = (bf16[256,1024]{1,0:T(8,128)(2,1)}, bf16[256,1024]{1,0:T(8,128)(2,1)}, u32[]{:S(2)}, u32[]{:S(2)}) collective-permute-start(bf16[256,1024]{1,0:T(8,128)(2,1)} %pad_maximum_fusion.40), channel_id=1, source_target_pairs={{0,8},{2,10},{4,12},{6,14},{8,0},{10,2},{12,4},{14,6},{16,24},{18,... | collective-permute-start | bytes 1572872 | tf_op jit(solution)/shard_map/ppermute | solution.py:312
  490.3 73.3 %collective-permute-start.78 = (bf16[128,512]{1,0:T(8,128)(2,1)}, bf16[128,512]{1,0:T(8,128)(2,1)S(1)}, u32[]{:S(2)}, u32[]{:S(2)}) collective-permute-start(bf16[128,512]{1,0:T(8,128)(2,1)} %dynamic-slice_bitcast_fusion.25), channel_id=1, source_target_pairs={{0,16},{2,18},{4,20},{6,22},{8,24},{10,26},{12,28},{14,30},{16,0},... | collective-permute-start | bytes 393224 | tf_op jit(solution)/shard_map/ppermute | solution.py:312
  525.6 39.5 %collective-permute-start.86 = (bf16[128,512]{1,0:T(8,128)(2,1)}, bf16[128,512]{1,0:T(8,128)(2,1)}, u32[]{:S(2)}, u32[]{:S(2)}) collective-permute-start(bf16[128,512]{1,0:T(8,128)(2,1)} %dynamic-slice_bitcast_fusion.24), channel_id=1, source_target_pairs={{0,16},{2,18},{4,20},{6,22},{8,24},{10,26},{12,28},{14,30},{16,0},... | collective-permute-start | bytes 393224 | tf_op jit(solution)/shard_map/ppermute | solution.py:312
  527.1 150.4 %collective-permute-start.97 = (bf16[256,2048]{1,0:T(8,128)(2,1)}, bf16[256,2048]{1,0:T(8,128)(2,1)}, u32[]{:S(2)}, u32[]{:S(2)}) collective-permute-start(bf16[256,2048]{1,0:T(8,128)(2,1)} %pad_maximum_fusion.29), channel_id=1, source_target_pairs={{0,4},{2,6},{4,0},{6,2},{8,12},{10,14},{12,8},{14,10},{16,20},{18,... | collective-permute-start | bytes 3145736 | tf_op jit(solution)/shard_map/ppermute | solution.py:312
  544.7 143.8 %collective-permute-start.105 = (bf16[512,1024]{1,0:T(8,128)(2,1)}, bf16[512,1024]{1,0:T(8,128)(2,1)}, u32[]{:S(2)}, u32[]{:S(2)}) collective-permute-start(bf16[512,1024]{1,0:T(8,128)(2,1)} %pad_maximum_fusion.30), channel_id=1, source_target_pairs={{0,2},{2,0},{4,6},{6,4},{8,10},{10,8},{12,14},{14,12},{16,18},{18,... | collective-permute-start | bytes 3145736 | tf_op jit(solution)/shard_map/ppermute | solution.py:312
  555.1 26.7 %collective-permute-start.68 = (bf16[512,512]{1,0:T(8,128)(2,1)}, bf16[512,512]{1,0:T(8,128)(2,1)}, u32[]{:S(2)}, u32[]{:S(2)}) collective-permute-start(bf16[512,512]{1,0:T(8,128)(2,1)} %dynamic-slice_bitcast_fusion.8), channel_id=1, source_target_pairs={{0,2},{2,0},{4,6},{6,4},{8,10},{10,8},{12,14},{14,12},{16,18},{18,... | collective-permute-start | bytes 1572872 | tf_op jit(solution)/shard_map/ppermute | solution.py:312
  563.6 27.1 %collective-permute-start.60 = (bf16[512,512]{1,0:T(8,128)(2,1)S(1)}, bf16[512,512]{1,0:T(8,128)(2,1)S(1)}, u32[]{:S(2)}, u32[]{:S(2)}) collective-permute-start(bf16[512,512]{1,0:T(8,128)(2,1)S(1)} %dynamic-slice_bitcast_fusion.9), channel_id=1, source_target_pairs={{0,4},{2,6},{4,0},{6,2},{8,12},{10,14},{12,8},{14,10},{16,20},{18,... | collective-permute-start | bytes 1572872 | tf_op jit(solution)/shard_map/ppermute | solution.py:312
  587.8 39.4 %collective-permute-start.39 = (bf16[256,2048]{1,0:T(8,128)(2,1)S(1)}, bf16[256,2048]{1,0:T(8,128)(2,1)S(1)}, u32[]{:S(2)}, u32[]{:S(2)}) collective-permute-start(bf16[256,2048]{1,0:T(8,128)(2,1)S(1)} %copy-done.153), channel_id=1, source_target_pairs={{0,4},{2,6},{4,0},{6,2},{8,12},{10,14},{12,8},{14,10},{16,20},{18,... | collective-permute-start | bytes 3145736 | tf_op jit(solution)/shard_map/ppermute | solution.py:312
  590.6 33.4 %collective-permute-start.20 = (bf16[512,1024]{1,0:T(8,128)(2,1)S(1)}, bf16[512,1024]{1,0:T(8,128)(2,1)S(1)}, u32[]{:S(2)}, u32[]{:S(2)}) collective-permute-start(bf16[512,1024]{1,0:T(8,128)(2,1)S(1)} %copy-done.165), channel_id=1, source_target_pairs={{0,1},{1,0},{2,3},{3,2},{4,5},{5,4},{6,7},{7,6},{8,9},{9,8},{10,11... | collective-permute-start | bytes 3145736 | tf_op jit(solution)/shard_map/ppermute | solution.py:70
  623.4 57.0 %collective-permute-start.30 = (bf16[1024,512]{1,0:T(8,128)(2,1)S(1)}, bf16[1024,512]{1,0:T(8,128)(2,1)S(1)}, u32[]{:S(2)}, u32[]{:S(2)}) collective-permute-start(bf16[1024,512]{1,0:T(8,128)(2,1)S(1)} %copy-done.212), channel_id=1, source_target_pairs={{0,4},{2,6},{4,0},{6,2},{8,12},{10,14},{12,8},{14,10},{16,20},{18,... | collective-permute-start | bytes 3145736 | tf_op jit(solution)/shard_map/ppermute | solution.py:312
  624.1 35.6 %collective-permute-start.81 = (bf16[512,512]{1,0:T(8,128)(2,1)S(1)}, bf16[512,512]{1,0:T(8,128)(2,1)S(1)}, u32[]{:S(2)}, u32[]{:S(2)}) collective-permute-start(bf16[512,512]{1,0:T(8,128)(2,1)S(1)} %pad_maximum_fusion.37), channel_id=1, source_target_pairs={{0,4},{2,6},{4,0},{6,2},{8,12},{10,14},{12,8},{14,10},{16,20},{18,... | collective-permute-start | bytes 1572872 | tf_op jit(solution)/shard_map/ppermute | solution.py:312
  627.3 40.3 %collective-permute-start.89 = (bf16[512,512]{1,0:T(8,128)(2,1)S(1)}, bf16[512,512]{1,0:T(8,128)(2,1)S(1)}, u32[]{:S(2)}, u32[]{:S(2)}) collective-permute-start(bf16[512,512]{1,0:T(8,128)(2,1)S(1)} %pad_maximum_fusion.38), channel_id=1, source_target_pairs={{0,2},{2,0},{4,6},{6,4},{8,10},{10,8},{12,14},{14,12},{16,18},{18,... | collective-permute-start | bytes 1572872 | tf_op jit(solution)/shard_map/ppermute | solution.py:312
  666.4 26.3 %collective-permute-start.22 = (bf16[1024,512]{1,0:T(8,128)(2,1)}, bf16[1024,512]{1,0:T(8,128)(2,1)}, u32[]{:S(2)}, u32[]{:S(2)}) collective-permute-start(bf16[1024,512]{1,0:T(8,128)(2,1)} %get-tuple-element.257), channel_id=1, source_target_pairs={{0,2},{2,0},{4,6},{6,4},{8,10},{10,8},{12,14},{14,12},{16,18},{18,... | collective-permute-start | bytes 3145736 | tf_op jit(solution)/shard_map/ppermute | solution.py:312
  676.0 39.3 %collective-permute-start.47 = (bf16[512,1024]{1,0:T(8,128)(2,1)}, bf16[512,1024]{1,0:T(8,128)(2,1)}, u32[]{:S(2)}, u32[]{:S(2)}) collective-permute-start(bf16[512,1024]{1,0:T(8,128)(2,1)} %dynamic-slice_bitcast_fusion.2), channel_id=1, source_target_pairs={{0,2},{2,0},{4,6},{6,4},{8,10},{10,8},{12,14},{14,12},{16,18},{18,... | collective-permute-start | bytes 3145736 | tf_op jit(solution)/shard_map/ppermute | solution.py:312
  677.5 207.7 %collective-permute-start.82 = (bf16[1024,512]{1,0:T(8,128)(2,1)}, bf16[1024,512]{1,0:T(8,128)(2,1)}, u32[]{:S(2)}, u32[]{:S(2)}) collective-permute-start(bf16[1024,512]{1,0:T(8,128)(2,1)} %pad_maximum_fusion.27), channel_id=1, source_target_pairs={{0,2},{2,0},{4,6},{6,4},{8,10},{10,8},{12,14},{14,12},{16,18},{18,... | collective-permute-start | bytes 3145736 | tf_op jit(solution)/shard_map/ppermute | solution.py:312
  680.4 169.3 %collective-permute-start.90 = (bf16[1024,512]{1,0:T(8,128)(2,1)}, bf16[1024,512]{1,0:T(8,128)(2,1)}, u32[]{:S(2)}, u32[]{:S(2)}) collective-permute-start(bf16[1024,512]{1,0:T(8,128)(2,1)} %pad_maximum_fusion.28), channel_id=1, source_target_pairs={{0,4},{2,6},{4,0},{6,2},{8,12},{10,14},{12,8},{14,10},{16,20},{18,... | collective-permute-start | bytes 3145736 | tf_op jit(solution)/shard_map/ppermute | solution.py:312
  688.5 84.1 %collective-permute-start.31 = (bf16[512,512]{1,0:T(8,128)(2,1)S(1)}, bf16[512,512]{1,0:T(8,128)(2,1)S(1)}, u32[]{:S(2)}, u32[]{:S(2)}) collective-permute-start(bf16[512,512]{1,0:T(8,128)(2,1)S(1)} %dynamic-slice_bitcast_fusion.12), channel_id=1, source_target_pairs={{0,2},{2,0},{4,6},{6,4},{8,10},{10,8},{12,14},{14,12},{16,18},{18,... | collective-permute-start | bytes 1572872 | tf_op jit(solution)/shard_map/ppermute | solution.py:312
  692.8 65.5 %collective-permute-start.72 = (bf16[256,512]{1,0:T(8,128)(2,1)S(1)}, bf16[256,512]{1,0:T(8,128)(2,1)S(1)}, u32[]{:S(2)}, u32[]{:S(2)}) collective-permute-start(bf16[256,512]{1,0:T(8,128)(2,1)S(1)} %copy-done.176), channel_id=1, source_target_pairs={{0,8},{2,10},{4,12},{6,14},{8,0},{10,2},{12,4},{14,6},{16,24},{18,... | collective-permute-start | bytes 786440 | tf_op jit(solution)/shard_map/ppermute | solution.py:312
  720.3 28.6 %collective-permute-start.55 = (f32[14,1024]{1,0:T(8,128)S(1)}, f32[14,1024]{1,0:T(8,128)S(1)}, u32[]{:S(2)}, u32[]{:S(2)}) collective-permute-start(f32[14,1024]{1,0:T(8,128)S(1)} %add.616), channel_id=1, source_target_pairs={{0,2},{2,0},{4,6},{6,4},{8,10},{10,8},{12,14},{14,12},{16,18},{18,... | collective-permute-start | bytes 172040 | tf_op jit(solution)/shard_map/ppermute | solution.py:369
  758.1 16.4 %collective-permute-start.23 = (bf16[512,512]{1,0:T(8,128)(2,1)S(1)}, bf16[512,512]{1,0:T(8,128)(2,1)S(1)}, u32[]{:S(2)}, u32[]{:S(2)}) collective-permute-start(bf16[512,512]{1,0:T(8,128)(2,1)S(1)} %dynamic-slice_bitcast_fusion.13), channel_id=1, source_target_pairs={{0,4},{2,6},{4,0},{6,2},{8,12},{10,14},{12,8},{14,10},{16,20},{18,... | collective-permute-start | bytes 1572872 | tf_op jit(solution)/shard_map/ppermute | solution.py:312
  771.1 14.8 %collective-permute-start.48 = (bf16[256,1024]{1,0:T(8,128)(2,1)S(1)}, bf16[256,1024]{1,0:T(8,128)(2,1)S(1)}, u32[]{:S(2)}, u32[]{:S(2)}) collective-permute-start(bf16[256,1024]{1,0:T(8,128)(2,1)S(1)} %dynamic-slice_bitcast_fusion.10), channel_id=1, source_target_pairs={{0,8},{2,10},{4,12},{6,14},{8,0},{10,2},{12,4},{14,6},{16,24},{18,... | collective-permute-start | bytes 1572872 | tf_op jit(solution)/shard_map/ppermute | solution.py:312
  772.6 23.7 %collective-permute-start.40 = (bf16[128,2048]{1,0:T(8,128)(2,1)S(1)}, bf16[128,2048]{1,0:T(8,128)(2,1)S(1)}, u32[]{:S(2)}, u32[]{:S(2)}) collective-permute-start(bf16[128,2048]{1,0:T(8,128)(2,1)S(1)} %copy-done.172), channel_id=1, source_target_pairs={{0,8},{2,10},{4,12},{6,14},{8,0},{10,2},{12,4},{14,6},{16,24},{18,... | collective-permute-start | bytes 1572872 | tf_op jit(solution)/shard_map/ppermute | solution.py:312
  774.5 31.2 %collective-permute-start.73 = (bf16[512,512]{1,0:T(8,128)(2,1)S(1)}, bf16[512,512]{1,0:T(8,128)(2,1)S(1)}, u32[]{:S(2)}, u32[]{:S(2)}) collective-permute-start(bf16[512,512]{1,0:T(8,128)(2,1)S(1)} %pad_maximum_fusion.36), channel_id=1, source_target_pairs={{0,2},{2,0},{4,6},{6,4},{8,10},{10,8},{12,14},{14,12},{16,18},{18,... | collective-permute-start | bytes 1572872 | tf_op jit(solution)/shard_map/ppermute | solution.py:312
  799.1 158.2 %collective-permute-start.98 = (bf16[512,2048]{1,0:T(8,128)(2,1)}, bf16[512,2048]{1,0:T(8,128)(2,1)}, u32[]{:S(2)}, u32[]{:S(2)}) collective-permute-start(bf16[512,2048]{1,0:T(8,128)(2,1)} %pad_maximum_fusion.13), channel_id=1, source_target_pairs={{0,2},{2,0},{4,6},{6,4},{8,10},{10,8},{12,14},{14,12},{16,18},{18,... | collective-permute-start | bytes 6291464 | tf_op jit(solution)/shard_map/ppermute | solution.py:312
  805.2 15.8 %collective-permute-start.65 = (bf16[512,512]{1,0:T(8,128)(2,1)S(1)}, bf16[512,512]{1,0:T(8,128)(2,1)S(1)}, u32[]{:S(2)}, u32[]{:S(2)}) collective-permute-start(bf16[512,512]{1,0:T(8,128)(2,1)S(1)} %pad_maximum_fusion.35), channel_id=1, source_target_pairs={{0,4},{2,6},{4,0},{6,2},{8,12},{10,14},{12,8},{14,10},{16,20},{18,... | collective-permute-start | bytes 1572872 | tf_op jit(solution)/shard_map/ppermute | solution.py:312
  805.7 14.6 %collective-permute-start.49 = (bf16[128,1024]{1,0:T(8,128)(2,1)S(1)}, bf16[128,1024]{1,0:T(8,128)(2,1)S(1)}, u32[]{:S(2)}, u32[]{:S(2)}) collective-permute-start(bf16[128,1024]{1,0:T(8,128)(2,1)S(1)} %dynamic-slice_bitcast_fusion.20), channel_id=1, source_target_pairs={{0,16},{2,18},{4,20},{6,22},{8,24},{10,26},{12,28},{14,30},{16,0},... | collective-permute-start | bytes 786440 | tf_op jit(solution)/shard_map/ppermute | solution.py:312
  820.4 132.4 %collective-permute-start.106 = (bf16[1024,1024]{1,0:T(8,128)(2,1)}, bf16[1024,1024]{1,0:T(8,128)(2,1)}, u32[]{:S(2)}, u32[]{:S(2)}) collective-permute-start(bf16[1024,1024]{1,0:T(8,128)(2,1)} %pad_maximum_fusion.14), channel_id=1, source_target_pairs={{0,4},{2,6},{4,0},{6,2},{8,12},{10,14},{12,8},{14,10},{16,20},{18,... | collective-permute-start | bytes 6291464 | tf_op jit(solution)/shard_map/ppermute | solution.py:312
  849.7 23.8 %collective-permute-start.50 = (bf16[128,1024]{1,0:T(8,128)(2,1)S(1)}, bf16[128,1024]{1,0:T(8,128)(2,1)S(1)}, u32[]{:S(2)}, u32[]{:S(2)}) collective-permute-start(bf16[128,1024]{1,0:T(8,128)(2,1)S(1)} %bitcast_add_fusion.20), channel_id=1, source_target_pairs={{0,16},{2,18},{4,20},{6,22},{8,24},{10,26},{12,28},{14,30},{16,0},... | collective-permute-start | bytes 786440 | tf_op jit(solution)/shard_map/ppermute | solution.py:312
  849.7 14.2 %collective-permute-start.34 = (bf16[128,512]{1,0:T(8,128)(2,1)S(1)}, bf16[128,512]{1,0:T(8,128)(2,1)S(1)}, u32[]{:S(2)}, u32[]{:S(2)}) collective-permute-start(bf16[128,512]{1,0:T(8,128)(2,1)S(1)} %bitcast_add_fusion.28), channel_id=1, source_target_pairs={{0,16},{2,18},{4,20},{6,22},{8,24},{10,26},{12,28},{14,30},{16,0},... | collective-permute-start | bytes 393224 | tf_op jit(solution)/shard_map/ppermute | solution.py:312
  872.5 65.6 %collective-permute-start.74 = (bf16[1024,512]{1,0:T(8,128)(2,1)}, bf16[1024,512]{1,0:T(8,128)(2,1)}, u32[]{:S(2)}, u32[]{:S(2)}) collective-permute-start(bf16[1024,512]{1,0:T(8,128)(2,1)} %pad_maximum_fusion.26), channel_id=1, source_target_pairs={{0,4},{2,6},{4,0},{6,2},{8,12},{10,14},{12,8},{14,10},{16,20},{18,... | collective-permute-start | bytes 3145736 | tf_op jit(solution)/shard_map/ppermute | solution.py:312
  893.2 14.3 %collective-permute-start.43 = (bf16[128,2048]{1,0:T(8,128)(2,1)S(1)}, bf16[128,2048]{1,0:T(8,128)(2,1)S(1)}, u32[]{:S(2)}, u32[]{:S(2)}) collective-permute-start(bf16[128,2048]{1,0:T(8,128)(2,1)S(1)} %pad_maximum_fusion.33), channel_id=1, source_target_pairs={{0,8},{2,10},{4,12},{6,14},{8,0},{10,2},{12,4},{14,6},{16,24},{18,... | collective-permute-start | bytes 1572872 | tf_op jit(solution)/shard_map/ppermute | solution.py:312
  898.8 14.3 %collective-permute-start.51 = (bf16[256,1024]{1,0:T(8,128)(2,1)S(1)}, bf16[256,1024]{1,0:T(8,128)(2,1)S(1)}, u32[]{:S(2)}, u32[]{:S(2)}) collective-permute-start(bf16[256,1024]{1,0:T(8,128)(2,1)S(1)} %pad_maximum_fusion.34), channel_id=1, source_target_pairs={{0,8},{2,10},{4,12},{6,14},{8,0},{10,2},{12,4},{14,6},{16,24},{18,... | collective-permute-start | bytes 1572872 | tf_op jit(solution)/shard_map/ppermute | solution.py:312
  907.5 14.8 %collective-permute-start.36 = (bf16[512,512]{1,0:T(8,128)(2,1)S(1)}, bf16[512,512]{1,0:T(8,128)(2,1)S(1)}, u32[]{:S(2)}, u32[]{:S(2)}) collective-permute-start(bf16[512,512]{1,0:T(8,128)(2,1)S(1)} %pad_maximum_fusion.32), channel_id=1, source_target_pairs={{0,2},{2,0},{4,6},{6,4},{8,10},{10,8},{12,14},{14,12},{16,18},{18,... | collective-permute-start | bytes 1572872 | tf_op jit(solution)/shard_map/ppermute | solution.py:312
  913.1 31.6 %collective-permute-start.66 = (bf16[1024,512]{1,0:T(8,128)(2,1)S(1)}, bf16[1024,512]{1,0:T(8,128)(2,1)S(1)}, u32[]{:S(2)}, u32[]{:S(2)}) collective-permute-start(bf16[1024,512]{1,0:T(8,128)(2,1)S(1)} %copy-done.162), channel_id=1, source_target_pairs={{0,2},{2,0},{4,6},{6,4},{8,10},{10,8},{12,14},{14,12},{16,18},{18,... | collective-permute-start | bytes 3145736 | tf_op jit(solution)/shard_map/ppermute | solution.py:312
  922.3 14.8 %collective-permute-start.28 = (bf16[512,512]{1,0:T(8,128)(2,1)S(1)}, bf16[512,512]{1,0:T(8,128)(2,1)S(1)}, u32[]{:S(2)}, u32[]{:S(2)}) collective-permute-start(bf16[512,512]{1,0:T(8,128)(2,1)S(1)} %pad_maximum_fusion.31), channel_id=1, source_target_pairs={{0,4},{2,6},{4,0},{6,2},{8,12},{10,14},{12,8},{14,10},{16,20},{18,... | collective-permute-start | bytes 1572872 | tf_op jit(solution)/shard_map/ppermute | solution.py:312
  937.1 33.4 %collective-permute-start.52 = (bf16[512,1024]{1,0:T(8,128)(2,1)}, bf16[512,1024]{1,0:T(8,128)(2,1)}, u32[]{:S(2)}, u32[]{:S(2)}) collective-permute-start(bf16[512,1024]{1,0:T(8,128)(2,1)} %pad_maximum_fusion.24), channel_id=1, source_target_pairs={{0,2},{2,0},{4,6},{6,4},{8,10},{10,8},{12,14},{14,12},{16,18},{18,... | collective-permute-start | bytes 3145736 | tf_op jit(solution)/shard_map/ppermute | solution.py:312
  938.1 23.8 %collective-permute-start.44 = (bf16[256,2048]{1,0:T(8,128)(2,1)}, bf16[256,2048]{1,0:T(8,128)(2,1)}, u32[]{:S(2)}, u32[]{:S(2)}) collective-permute-start(bf16[256,2048]{1,0:T(8,128)(2,1)} %pad_maximum_fusion.23), channel_id=1, source_target_pairs={{0,4},{2,6},{4,0},{6,2},{8,12},{10,14},{12,8},{14,10},{16,20},{18,... | collective-permute-start | bytes 3145736 | tf_op jit(solution)/shard_map/ppermute | solution.py:312
  944.7 39.7 %collective-permute-start.37 = (bf16[1024,512]{1,0:T(8,128)(2,1)}, bf16[1024,512]{1,0:T(8,128)(2,1)}, u32[]{:S(2)}, u32[]{:S(2)}) collective-permute-start(bf16[1024,512]{1,0:T(8,128)(2,1)} %pad_maximum_fusion.22), channel_id=1, source_target_pairs={{0,4},{2,6},{4,0},{6,2},{8,12},{10,14},{12,8},{14,10},{16,20},{18,... | collective-permute-start | bytes 3145736 | tf_op jit(solution)/shard_map/ppermute | solution.py:312
  952.8 38.0 %collective-permute-start.29 = (bf16[1024,512]{1,0:T(8,128)(2,1)}, bf16[1024,512]{1,0:T(8,128)(2,1)}, u32[]{:S(2)}, u32[]{:S(2)}) collective-permute-start(bf16[1024,512]{1,0:T(8,128)(2,1)} %pad_maximum_fusion.21), channel_id=1, source_target_pairs={{0,2},{2,0},{4,6},{6,4},{8,10},{10,8},{12,14},{14,12},{16,18},{18,... | collective-permute-start | bytes 3145736 | tf_op jit(solution)/shard_map/ppermute | solution.py:312
  965.2 60.5 %collective-permute-start.45 = (bf16[512,2048]{1,0:T(8,128)(2,1)}, bf16[512,2048]{1,0:T(8,128)(2,1)}, u32[]{:S(2)}, u32[]{:S(2)}) collective-permute-start(bf16[512,2048]{1,0:T(8,128)(2,1)} %pad_maximum_fusion.11), channel_id=1, source_target_pairs={{0,2},{2,0},{4,6},{6,4},{8,10},{10,8},{12,14},{14,12},{16,18},{18,... | collective-permute-start | bytes 6291464 | tf_op jit(solution)/shard_map/ppermute | solution.py:312
  973.9 59.0 %collective-permute-start.53 = (bf16[1024,1024]{1,0:T(8,128)(2,1)}, bf16[1024,1024]{1,0:T(8,128)(2,1)}, u32[]{:S(2)}, u32[]{:S(2)}) collective-permute-start(bf16[1024,1024]{1,0:T(8,128)(2,1)} %pad_maximum_fusion.12), channel_id=1, source_target_pairs={{0,4},{2,6},{4,0},{6,2},{8,12},{10,14},{12,8},{14,10},{16,20},{18,... | collective-permute-start | bytes 6291464 | tf_op jit(solution)/shard_map/ppermute | solution.py:312
  (272 other events, 2735.6 us)
